TPU v7x, 32 devices: a whole 2x2x4 slice. The times are simulated.
32 devices in a mesh: groups: 2 (over x), long: 16 (over z, y, core).
Axes of the slice: x: 2, y: 2, z: 4, core: 2. Of those that a mesh axis runs over, the one named last changes fastest.
Arguments:
- displacement: float32 [4, 2, 128, 16, 256], P('groups', None, 'long'), parts along dimension 0, may hold values from -6 to 6
- velocity: float32 [4, 2, 128, 16, 256], P('groups', None, 'long'), parts along dimension 0, may hold values from -4 to 4
- damage: float32 [4, 128, 16, 256], P('groups', 'long'), parts along dimension 0, may hold values from 0 to 0.6
- material: int32 [4, 128, 16, 256], P('groups', 'long'), parts along dimension 0, may hold values from 0 to 3
- damage_table: float32 [2, 4], replicated, may hold values from 0.1 to 2
- fault_rows: int32 [4, 128, 16], P('groups', 'long'), parts along dimension 0, may hold values from 0 to 3
- kernel: float32 [16, 64, 2, 2], P(None, 'long'), may hold values from -1.5 to 1.5
- history: float32 [30, 64, 2, 2, 16], P('groups', 'long'), parts along dimension 0, may hold values from -6 to 6
Outputs:
- displacement_out: float32 [4, 2, 128, 16, 256], P('groups', None, 'long'), parts along dimension 0
- velocity_out: float32 [4, 2, 128, 16, 256], P('groups', None, 'long'), parts along dimension 0
- damage_out: float32 [4, 128, 16, 256], P('groups', 'long'), parts along dimension 0
- history_out: float32 [30, 64, 2, 2, 16], P('groups', 'long'), parts along dimension 0
There are 2 independent parts, one for each index of `groups`. A program takes and returns all parts, laid end to end along the dimension named above; an argument that names none is the same for every part. Nothing has to cross between parts.
Inputs may be any that keep to these rules, and one draw needn't show every extreme that they name: `fault_rows`: row of the fault face, counted from the fault.
All inputs are finite; a program needn't handle non-finite values.
Results may differ from a plain program's by a relative error of at most 0.00011.
Values sent between devices are 32-bit elements; how exact they have to be, the bound alone decides.
A program may use at most 64 MiB of HBM per device.

v0:
```python
import math

import jax
import jax.numpy as jnp
from jax import lax
from jax.sharding import PartitionSpec as P

STEPS = 2


time_step = 0.5


def padded_2(block, sides, width):
    for axis, dim in sides:
        count = lax.axis_size(axis)
        forward = [(i, i + 1) for i in range(count - 1)]
        forward.append((count - 1, 0))
        backward = [(target, source) for source, target in forward]
        low = lax.ppermute(
            lax.slice_in_dim(block, block.shape[dim] - width, None, axis=dim), axis, forward
        )
        high = lax.ppermute(lax.slice_in_dim(block, 0, width, axis=dim), axis, backward)
        block = jnp.concatenate([low, block, high], axis=dim)
    return block


def class_lookup(material, table_row):
    result = jnp.zeros(material.shape, table_row.dtype)
    for level in range(table_row.shape[0]):
        result = result + jnp.where(
            material == level, table_row[level], jnp.zeros((), table_row.dtype)
        )
    return result


def neighbour(values_in, axis, higher):
    selector = [slice(None)] * values_in.ndim
    for dimension in range(values_in.ndim - 3, values_in.ndim):
        selector[dimension] = slice(1, -1)
    selector[axis] = slice(2, None) if higher else slice(0, -2)
    return values_in[tuple(selector)]


def local_terms(padded_u, padded_c):
    outer_u = jnp.pad(padded_u, ((0, 0), (0, 0), (0, 0), (1, 1), (1, 1)))
    outer_c = jnp.pad(padded_c, ((0, 0), (0, 0), (1, 1), (1, 1)), mode="edge")
    centre_u = outer_u[:, :, 1:-1, 1:-1, 1:-1]
    centre_c = outer_c[:, 1:-1, 1:-1, 1:-1]
    forces = jnp.zeros_like(centre_u)
    energy = jnp.zeros_like(centre_c)
    for offset in range(3):
        above_u = neighbour(outer_u, 2 + offset, True)
        below_u = neighbour(outer_u, 2 + offset, False)
        above_c = neighbour(outer_c, 1 + offset, True)
        below_c = neighbour(outer_c, 1 + offset, False)
        forces = forces + (0.5 * (centre_c + above_c))[None] * (above_u - centre_u)
        forces = forces + (0.5 * (centre_c + below_c))[None] * (below_u - centre_u)
        gradient = 0.5 * (above_u - below_u)
        energy = energy + jnp.sum(gradient * gradient, axis=0)
    return (forces, energy)


def convolve(kernel, stacked):
    kernel_real = kernel[:, :, 0, :, None]
    kernel_imag = kernel[:, :, 1, :, None]
    spec_real = stacked[:, :, 0]
    spec_imag = stacked[:, :, 1]
    out_real = jnp.sum(kernel_real * spec_real - kernel_imag * spec_imag, axis=0)
    out_imag = jnp.sum(kernel_real * spec_imag + kernel_imag * spec_real, axis=0)
    return (out_real, out_imag)


def basis(waves, places, length):
    phase = (waves[:, None] * places[None, :] % length).astype(jnp.float32) * (
        2.0 * math.pi / length
    )
    return (jnp.cos(phase), jnp.sin(phase))


def spectral_terms(cosine, sine_table, slip_part, norming):
    part_real = (
        jnp.einsum("kx,cxz->kcz", cosine, slip_part, precision=lax.Precision.HIGHEST) * norming
    )
    part_imag = (
        -jnp.einsum("kx,cxz->kcz", sine_table, slip_part, precision=lax.Precision.HIGHEST) * norming
    )
    return jnp.stack([part_real, part_imag], 1)


def wave_sum(waves, places, spectrum, length, norming):
    cosine, sine_table = basis(waves, places, length)
    weights = jnp.where(waves == 0, 1.0, 2.0).astype(jnp.float32) * norming
    first_part = jnp.einsum(
        "kx,kcz->cxz", cosine * weights[:, None], spectrum[:, 0], precision=lax.Precision.HIGHEST
    )
    second_part = jnp.einsum(
        "kx,kcz->cxz",
        sine_table * weights[:, None],
        spectrum[:, 1],
        precision=lax.Precision.HIGHEST,
    )
    return first_part - second_part


def advance(
    disp_mid, vel_mid, dmg_mid, rate_mid, limit_mid, fault_mid, forces, energy, traction, signs
):
    pushes = traction[:, None, :, :, None] * signs[None] * fault_mid[None]
    vel_new = vel_mid + time_step * (forces + pushes)
    disp_new = disp_mid + time_step * vel_new
    dmg_new = 1.0 - (1.0 - dmg_mid) * jnp.exp(-rate_mid * jax.nn.softplus(energy - limit_mid))
    return (disp_new, vel_new, dmg_new)


def per_device(displacement, velocity, damage, material, damage_table, fault_rows, kernel, history):
    cells = displacement.shape[2]
    position = lax.axis_index("long")
    length = cells * lax.axis_size("long")
    owned = cells // 2
    norming = 1.0 / math.sqrt(length)
    rates = class_lookup(material, damage_table[0])
    limits = class_lookup(material, damage_table[1])
    heights = lax.broadcasted_iota(jnp.int32, damage.shape, 3)
    on_fault = (heights == fault_rows[..., None]).astype(displacement.dtype)
    signs = jnp.array([1.0, -1.0], displacement.dtype)[:, None, None, None]
    lagged = [history[level] for level in range(history.shape[0])]
    for number in range(STEPS):
        stiffness = 1.0 - damage
        stacked_fields = jnp.concatenate([displacement, stiffness[None]], 0)
        padded = padded_2(stacked_fields, (("long", 2),), 1)
        forces, energy = local_terms(padded[:-1], padded[-1])
        own_disp = displacement
        face = jnp.sum(own_disp * on_fault[None], axis=4)
        slip = face[:, 1] - face[:, 0]
        waves = jnp.arange(lax.axis_size("long") * owned, dtype=jnp.int32)
        places = position * cells + jnp.arange(cells, dtype=jnp.int32)
        cosine, sine_table = basis(waves, places, length)
        current = lax.psum_scatter(
            spectral_terms(cosine, sine_table, slip, norming),
            "long",
            scatter_dimension=0,
            tiled=True,
        )
        stacked_lags = jnp.stack([current] + lagged, 0)
        traction_real, traction_imag = convolve(kernel, stacked_lags)
        traction_spectrum = jnp.stack([traction_real, traction_imag], 1)

        def add_waves(piece):
            waves = jnp.arange(piece.shape[0], dtype=jnp.int32)
            places = position * cells + jnp.arange(cells, dtype=jnp.int32)
            return wave_sum(waves, places, piece, length, norming)

        traction = add_waves(lax.all_gather(traction_spectrum, "long", axis=0, tiled=True))
        displacement, velocity, damage = advance(
            displacement, velocity, damage, rates, limits, on_fault, forces, energy, traction, signs
        )
        lagged = [current] + lagged[:-1]
    return (displacement, velocity, damage, jnp.stack(lagged, 0))


def solution(mesh):
    placed = (
        P("groups", None, "long", None, None),
        P("groups", None, "long", None, None),
        P("groups", "long", None, None),
        P("groups", "long", None, None),
        P(),
        P("groups", "long", None),
        P(None, "long", None, None),
        P("groups", "long", None, None, None),
    )
    return jax.shard_map(
        per_device,
        mesh=mesh,
        in_specs=placed,
        out_specs=(
            P("groups", None, "long", None, None),
            P("groups", None, "long", None, None),
            P("groups", "long", None, None),
            P("groups", "long", None, None, None),
        ),
        check_vma=False,
    )
```

profile of v0, /device:TPU:0, one launch (start us, length us, event | category | flops | bytes accessed | tf_op | source)
XLA Modules:
  0.0 214.8 jit_solution(16481410820871778354)
XLA Ops:
  0.7 1.0 subtract_bitcast_fusion
  1.7 0.9 pad_maximum_fusion.31
  3.1 5.1 %collective-permute-start.1 = (f32[3,2,1,16,256]{4,3,2,1,0:T(8,128)S(1)}, f32[3,2,1,16,256]{4,3,2,1,0:T(8,128)S(1)}, u32[]{:S(2)}, u32[]{:S(2)}) collective-permute-start(f32[3,2,1,16,256]{4,3,2,1,0:T(8,128)S(1)} %get-tuple-element.28), channel_id=1, source_target_pairs={{1,0},{2,1},{3,2},{4,3},{5,4},{6,5},{7,6},{8,7},{9,8},{10,9},{11,1... | collective-permute-start | bytes 294920 | tf_op jit(solution)/shard_map/ppermute | solution.py:23
  11.5 1.4 multiply_reduce_fusion.5
  14.3 0.9 fusion.122
  15.3 62.3 %all-reduce.2 = f32[64,2,2,16]{3,2,1,0:T(2,128)S(1)} all-reduce(f32[64,2,2,16]{3,2,1,0:T(2,128)S(1)} %copy.50), channel_id=2, replica_groups=mesh['groups'=2,'long'=16] {'long'}, use_global_device_ids=true, to_apply=%region_1.2.clone | all-reduce | flops 4096 | bytes 32768
  77.9 17.5 %all_gather.6 = f32[64,2,2,16]{3,2,1,0:T(2,128)S(1)} all-gather(f32[4,2,2,16]{3,2,1,0:T(2,128)S(1)} %copy.54), channel_id=1, replica_groups=mesh['groups'=2,'long'=16] {'long'}, dimensions={0}, use_global_device_ids=true | all-gather | bytes 17408 | tf_op jit(solution)/shard_map/all_gather | solution.py:154
  95.6 1.5 fusion.33
  97.8 6.1 %fusion.15 = (f32[2,8,16,256]{3,2,1,0:T(8,128)S(1)}, pred[2,8,16,256]{3,2,1,0:T(8,128)(4,1)}, pred[2,8,16,256]{3,2,1,0:T(8,128)(4,1)}, pred[2,8,16,256]{3,2,1,0:T(8,128)(4,1)}, pred[2,8,16,256]{3,2,1,0:T(8,128)(4,1)}) fusion(f32[2,8,16,256]{3,2,1,0:T(8,128)S(1)} %copy-done.5, f32[2,8,16,256]{3,2,1,0:T(8,128)S(1)} %copy-done.6, ...), kind=kLoop, calls=%fused_computation.57 | loop fusion | flops 2162688 | bytes 1835040 | tf_op jit(solution)/shard_map/sub | solution.py:129
  104.0 1.5 multiply_add_fusion.2
  105.9 4.1 %collective-permute-start.3 = (f32[3,2,1,16,256]{4,3,2,1,0:T(8,128)S(1)}, f32[3,2,1,16,256]{4,3,2,1,0:T(8,128)S(1)}, u32[]{:S(2)}, u32[]{:S(2)}) collective-permute-start(f32[3,2,1,16,256]{4,3,2,1,0:T(8,128)S(1)} %get-tuple-element.26), channel_id=1, source_target_pairs={{1,0},{2,1},{3,2},{4,3},{5,4},{6,5},{7,6},{8,7},{9,8},{10,9},{11,1... | collective-permute-start | bytes 294920 | tf_op jit(solution)/shard_map/ppermute | solution.py:23
  110.7 1.8 collective-permute-done.2
  113.2 0.9 multiply_reduce_fusion.2
  115.1 1.3 multiply_reduce_fusion.1
  117.2 0.8 copy.57
  118.0 63.8 %all-reduce.3 = f32[64,2,2,16]{3,2,1,0:T(2,128)} all-reduce(f32[64,2,2,16]{3,2,1,0:T(2,128)} %copy.57), channel_id=3, replica_groups=mesh['groups'=2,'long'=16] {'long'}, use_global_device_ids=true, to_apply=%region_8.9.clone | all-reduce | flops 4096 | bytes 32768
  182.8 17.5 %all_gather.7 = f32[64,2,2,16]{3,2,1,0:T(2,128)S(1)} all-gather(f32[4,2,2,16]{3,2,1,0:T(2,128)S(1)} %copy.61), channel_id=1, replica_groups=mesh['groups'=2,'long'=16] {'long'}, dimensions={0}, use_global_device_ids=true | all-gather | bytes 17408 | tf_op jit(solution)/shard_map/all_gather | solution.py:154
  200.9 0.9 copy.72
  201.8 0.9 fusion.45
  202.9 0.9 fusion.9
  203.9 1.7 pad_maximum_fusion.27
  205.6 1.3 fusion.23
  207.0 6.2 %fusion.19 = f32[2,8,16,256]{3,2,1,0:T(8,128)} fusion(f32[2,8,16,256]{3,2,1,0:T(8,128)S(1)} %get-tuple-element.18, f32[2,8,16,256]{3,2,1,0:T(8,128)S(1)} %copy-done.9, f32[2,8,16,256]{3,2,1,0:T(8,128)S(1)} %copy-done.10, f32[2,8,16,256]{3,2,1,0:T(8,128)S(1)} %copy-done.8, pred[2,8,16,256]{3,2,1,0:T(8,128)(4,1)S(1)} %copy-done.20, ...), kind=kLoop, calls=%fused_computation.61 | loop fusion | flops 1769472 | bytes 1572896 | tf_op jit(solution)/shard_map/sub | solution.py:112
  213.2 1.6 multiply_add_fusion
  (111 shorter events, 11.4 us)
Async XLA Ops:
  0.6 9.1 %copy-start.27 = (u32[32]{0:T(128)S(1)}, u32[32]{0:T(128)}, u32[]{:S(2)}) copy-start(u32[32]{0:T(128)} %constant.74) | copy-start | bytes 388
  0.6 10.4 %copy-start = (f32[2,2,8,16,256]{4,3,2,1,0:T(8,128)S(1)}, f32[2,2,8,16,256]{4,3,2,1,0:T(8,128)}, u32[]{:S(2)}) copy-start(f32[2,2,8,16,256]{4,3,2,1,0:T(8,128)} %param.9) | copy-start | bytes 1572868
  0.7 8.1 %copy-start.24 = (s32[2,8,16]{2,1,0:T(8,128)S(1)}, s32[2,8,16]{2,1,0:T(8,128)}, u32[]{:S(2)}) copy-start(s32[2,8,16]{2,1,0:T(8,128)} %param.14) | copy-start | bytes 3076
  0.7 8.2 %copy-start.23 = (f32[2,4]{1,0:T(2,128)S(1)}, f32[2,4]{1,0:T(2,128)}, u32[]{:S(2)}) copy-start(f32[2,4]{1,0:T(2,128)} %param.13) | copy-start | bytes 100
  0.7 8.8 %copy-start.25 = (f32[16,4,2,2]{0,3,2,1:T(2,128)S(1)}, f32[16,4,2,2]{0,3,2,1:T(2,128)}, u32[]{:S(2)}) copy-start(f32[16,4,2,2]{0,3,2,1:T(2,128)} %param.15) | copy-start | bytes 3076
  2.6 8.4 %collective-permute-start = (f32[3,2,1,16,256]{4,3,2,1,0:T(8,128)S(1)}, f32[3,2,1,16,256]{4,3,2,1,0:T(8,128)S(1)}, u32[]{:S(2)}, u32[]{:S(2)}) collective-permute-start(f32[3,2,1,16,256]{4,3,2,1,0:T(8,128)S(1)} %get-tuple-element.27), channel_id=1, source_target_pairs={{0,1},{1,2},{2,3},{3,4},{4,5},{5,6},{6,7},{7,8},{8,9},{9,10},{10,1... | collective-permute-start | bytes 294920 | tf_op jit(solution)/shard_map/ppermute | solution.py:20
  3.1 7.9 %collective-permute-start.1 = (f32[3,2,1,16,256]{4,3,2,1,0:T(8,128)S(1)}, f32[3,2,1,16,256]{4,3,2,1,0:T(8,128)S(1)}, u32[]{:S(2)}, u32[]{:S(2)}) collective-permute-start(f32[3,2,1,16,256]{4,3,2,1,0:T(8,128)S(1)} %get-tuple-element.28), channel_id=1, source_target_pairs={{1,0},{2,1},{3,2},{4,3},{5,4},{6,5},{7,6},{8,7},{9,8},{10,9},{11,1... | collective-permute-start | bytes 294920 | tf_op jit(solution)/shard_map/ppermute | solution.py:23
  9.7 67.9 %copy-start.14 = (f32[16,4,2]{2,1,0:T(4,128)}, f32[16,4,2]{2,1,0:T(4,128)S(1)}, u32[]{:S(2)}) copy-start(f32[16,4,2]{2,1,0:T(4,128)S(1)} %copy.53) | copy-start | bytes 1540
  13.5 64.1 %copy-start.11 = (f32[15,4,2,2,16]{4,3,2,1,0:T(2,128)S(1)}, f32[15,4,2,2,16]{4,3,2,1,0:T(2,128)}, u32[]{:S(2)}) copy-start(f32[15,4,2,2,16]{4,3,2,1,0:T(2,128)} %param.16) | copy-start | bytes 46084
  97.1 6.9 %copy-start.3 = (f32[2,8,16,256]{3,2,1,0:T(8,128)S(1)}, f32[2,8,16,256]{3,2,1,0:T(8,128)}, u32[]{:S(2)}) copy-start(f32[2,8,16,256]{3,2,1,0:T(8,128)} %fusion.38) | copy-start | bytes 786436
  97.1 6.9 %copy-start.13 = (f32[2,2,8,16,256]{4,3,2,1,0:T(8,128)S(1)}, f32[2,2,8,16,256]{4,3,2,1,0:T(8,128)}, u32[]{:S(2)}) copy-start(f32[2,2,8,16,256]{4,3,2,1,0:T(8,128)} %param.10) | copy-start | bytes 1572868
  104.0 6.0 %copy-start.12 = (f32[15,4,2,2,16]{4,3,2,1,0:T(2,128)S(1)}, f32[15,4,2,2,16]{4,3,2,1,0:T(2,128)}, u32[]{:S(2)}) copy-start(f32[15,4,2,2,16]{4,3,2,1,0:T(2,128)} %param.16) | copy-start | bytes 46084
  105.5 6.9 %collective-permute-start.2 = (f32[3,2,1,16,256]{4,3,2,1,0:T(8,128)S(1)}, f32[3,2,1,16,256]{4,3,2,1,0:T(8,128)S(1)}, u32[]{:S(2)}, u32[]{:S(2)}) collective-permute-start(f32[3,2,1,16,256]{4,3,2,1,0:T(8,128)S(1)} %get-tuple-element.25), channel_id=1, source_target_pairs={{0,1},{1,2},{2,3},{3,4},{4,5},{5,6},{6,7},{7,8},{8,9},{9,10},{10,1... | collective-permute-start | bytes 294920 | tf_op jit(solution)/shard_map/ppermute | solution.py:20
  105.9 6.5 %collective-permute-start.3 = (f32[3,2,1,16,256]{4,3,2,1,0:T(8,128)S(1)}, f32[3,2,1,16,256]{4,3,2,1,0:T(8,128)S(1)}, u32[]{:S(2)}, u32[]{:S(2)}) collective-permute-start(f32[3,2,1,16,256]{4,3,2,1,0:T(8,128)S(1)} %get-tuple-element.26), channel_id=1, source_target_pairs={{1,0},{2,1},{3,2},{4,3},{5,4},{6,5},{7,6},{8,7},{9,8},{10,9},{11,1... | collective-permute-start | bytes 294920 | tf_op jit(solution)/shard_map/ppermute | solution.py:23
  112.5 3.9 %copy-start.21 = (f32[2,10,1,256]{3,2,1,0:T(1,128)}, f32[2,10,1,256]{3,2,1,0:T(1,128)S(1)}, u32[]{:S(2)}) copy-start(f32[2,10,1,256]{3,2,1,0:T(1,128)S(1)} %get-tuple-element.43) | copy-start | bytes 61444
  112.5 3.9 %copy-start.22 = (f32[2,10,1,256]{3,2,1,0:T(1,128)}, f32[2,10,1,256]{3,2,1,0:T(1,128)S(1)}, u32[]{:S(2)}) copy-start(f32[2,10,1,256]{3,2,1,0:T(1,128)S(1)} %get-tuple-element.44) | copy-start | bytes 61444
  116.4 66.1 %slice-start = ((f32[15,4,2,2,16]{4,3,2,1,0:T(2,128)}), f32[14,4,2,2,16]{4,3,2,1,0:T(2,128)S(1)}, s32[]{:S(2)}) async-start(f32[15,4,2,2,16]{4,3,2,1,0:T(2,128)} %param.16), calls=%async_computation | async-start | bytes 229376 | tf_op jit(solution)/shard_map/slice | solution.py:127
  116.4 66.2 %copy-start.15 = (f32[16,4,2]{2,1,0:T(4,128)S(1)}, f32[16,4,2]{2,1,0:T(4,128)}, u32[]{:S(2)}) copy-start(f32[16,4,2]{2,1,0:T(4,128)} %copy-done.14) | copy-start | bytes 1540
  203.9 3.1 %copy-start.17 = (pred[2,8,16,256]{3,2,1,0:T(8,128)(4,1)S(1)}, pred[2,8,16,256]{3,2,1,0:T(8,128)(4,1)}, u32[]{:S(2)}) copy-start(pred[2,8,16,256]{3,2,1,0:T(8,128)(4,1)} %get-tuple-element.19) | copy-start | bytes 196612
  203.9 3.1 %copy-start.18 = (pred[2,8,16,256]{3,2,1,0:T(8,128)(4,1)S(1)}, pred[2,8,16,256]{3,2,1,0:T(8,128)(4,1)}, u32[]{:S(2)}) copy-start(pred[2,8,16,256]{3,2,1,0:T(8,128)(4,1)} %get-tuple-element.20) | copy-start | bytes 196612
  203.9 3.1 %copy-start.19 = (pred[2,8,16,256]{3,2,1,0:T(8,128)(4,1)S(1)}, pred[2,8,16,256]{3,2,1,0:T(8,128)(4,1)}, u32[]{:S(2)}) copy-start(pred[2,8,16,256]{3,2,1,0:T(8,128)(4,1)} %get-tuple-element.21) | copy-start | bytes 196612
  203.9 3.1 %copy-start.20 = (pred[2,8,16,256]{3,2,1,0:T(8,128)(4,1)S(1)}, pred[2,8,16,256]{3,2,1,0:T(8,128)(4,1)}, u32[]{:S(2)}) copy-start(pred[2,8,16,256]{3,2,1,0:T(8,128)(4,1)} %get-tuple-element.22) | copy-start | bytes 196612
  206.9 6.3 %copy-start.1 = (f32[2,2,8,16,256]{4,3,2,1,0:T(8,128)S(1)}, f32[2,2,8,16,256]{4,3,2,1,0:T(8,128)}, u32[]{:S(2)}) copy-start(f32[2,2,8,16,256]{4,3,2,1,0:T(8,128)} %get-tuple-element.24) | copy-start | bytes 1572868
  207.0 6.3 %copy-start.2 = (f32[2,8,16,256]{3,2,1,0:T(8,128)S(1)}, f32[2,8,16,256]{3,2,1,0:T(8,128)}, u32[]{:S(2)}) copy-start(f32[2,8,16,256]{3,2,1,0:T(8,128)} %fusion.28) | copy-start | bytes 786436
  (10 other events, 24.4 us)
where the time goes:
time: 215 us
  blocking collectives  161 us (75%)
  other arithmetic  29.3 us (14%)
  starting transfers between devices  10.1 us (5%)
  local copies, waits for them, and re-layouts  7.45 us (3%)
  matrix products  3.4 us (2%)
    unnamed x2, blocking collectives  126 us
    all_gather x2, blocking collectives, per_device(): lax.all_gather(traction_spectrum, 'long', axis=0, tiled=True)  35 us
    ppermute x2, starting transfers between devices, padded_2(): lax.ppermute(lax.slice_in_dim(block, 0, width, axis=dim), axis, backward)  9.16 us
    sub x1, other arithmetic, advance(): 1.0 - (1.0 - dmg_mid) * jnp.exp(-rate_mid * jax.nn.softplus(energy - limi...  6.16 us
    sub x1, other arithmetic, per_device(): stiffness = 1.0 - damage  6.15 us
  transfers between devices with their start and end apart: 4, of which 1 were waited for; matrix products, arithmetic and copies ran while one was open for 1% of the time, Pallas kernels for 0%

commit v1 on v0

v1 whole, which is shorter than its diff:
```python
import functools
import math

import jax
import jax.numpy as jnp
import numpy as np
from jax import lax
from jax.experimental import pallas as pl
from jax.experimental.pallas import tpu as pltpu
from jax.sharding import PartitionSpec as P

time_step = 0.5
MESH = pl.DeviceIdType.MESH
HIGHEST = lax.Precision.HIGHEST


def bases(length, cells):
    waves = np.arange(length // 2)
    places = np.arange(length)
    norming = 1.0 / math.sqrt(length)

    def table(k, x):
        phase = (k[:, None] * x[None, :] % length) * (2.0 * math.pi / length)
        return np.cos(phase) * norming, -np.sin(phase) * norming

    cosine, sine = table(waves, places)
    forward = np.stack([cosine, sine], 1).reshape(length, length)
    swapped = np.stack([sine, cosine], 1).reshape(length, length)
    cosine, sine = table(waves, np.arange(-cells, length + cells))
    weights = np.where(waves == 0, 1.0, 2.0)[:, None]
    inverse = np.stack([cosine * weights, sine * weights], 1).reshape(length, -1).T
    return np.concatenate([forward, swapped], 0).astype(np.float32), inverse.astype(np.float32)


def class_lookup(material, table_ref, row):
    count = table_ref.shape[1]
    result = jnp.full(material.shape, table_ref[row, count - 1])
    for level in range(count - 1):
        result = jnp.where(material == level, table_ref[row, level], result)
    return result


def body(
    n, disp_hbm, vel_hbm, dmg_hbm, mat_ref, table_ref, fault_ref, kr_ref, ki_ref, hist_ref,
    forward_ref, inverse_ref,
    disp_out, vel_out, dmg_out, hist_out,
    u1, u2, d1, d2, vel, face, gather1, gather2, spectra, push2,
    load_sems, halo_send, halo_recv, all_send, all_recv,
):
    cells = vel.shape[2]
    depth, rows = vel.shape[3], vel.shape[4]
    group = lax.axis_index("groups")
    me = lax.axis_index("long")
    left, right = lax.rem(me + n - 1, n), lax.rem(me + 1, n)
    dt = time_step

    barrier = pltpu.get_barrier_semaphore()

    @pl.loop(1, n)
    def _(step):
        pl.semaphore_signal(
            barrier, inc=1, device_id=(group, lax.rem(me + step, n)), device_id_type=MESH
        )

    loads = [
        pltpu.make_async_copy(disp_hbm, u1.at[:, :, pl.ds(1, cells)], load_sems.at[0]),
        pltpu.make_async_copy(dmg_hbm, d1.at[:, pl.ds(1, cells)], load_sems.at[1]),
        pltpu.make_async_copy(vel_hbm, vel, load_sems.at[2]),
    ]
    for copy in loads:
        copy.start()

    diagonal = lax.broadcasted_iota(jnp.int32, (depth, depth), 0) == lax.broadcasted_iota(
        jnp.int32, (depth, depth), 1
    )
    for s in range(2):
        rows_s = fault_ref[s].astype(jnp.float32)
        for x in range(cells):
            line = jnp.where(diagonal, rows_s[x : x + 1, :], 0.0)
            column = jnp.sum(line, axis=1, keepdims=True)
            face[s, x + 1] = jnp.broadcast_to(column, (depth, 128))

    lane = lax.broadcasted_iota(jnp.int32, (depth, 128), 1)
    lane_f = lane.astype(jnp.float32)
    lane8 = lax.broadcasted_iota(jnp.int32, (8, 128), 1)

    def slip_tile(u):
        parts = []
        for c in range(2):
            total = jnp.zeros((depth, 128), jnp.float32)
            for x in range(cells):
                on0 = jnp.where(lane_f == face[0, x + 1], u[c, 0, x + 1, :, :128], 0.0)
                on1 = jnp.where(lane_f == face[1, x + 1], u[c, 1, x + 1, :, :128], 0.0)
                column = jnp.sum(on1 - on0, axis=1, keepdims=True)
                total = jnp.where(lane == x, column, total)
            parts.append(total)
        parts.append(jnp.zeros((128 - 2 * depth, 128), jnp.float32))
        return jnp.concatenate(parts, 0).T[:cells, :]

    odd = lax.broadcasted_iota(jnp.int32, (cells, 128), 0) % 2 == 1

    def exchange(block):
        return jnp.where(odd, pltpu.roll(block, 1, 0), pltpu.roll(block, cells - 1, 0))

    lags = kr_ref.shape[0]
    sum1 = jnp.zeros((cells, 128), jnp.float32)
    sum2 = jnp.zeros((cells, 128), jnp.float32)
    for lag in range(1, lags):
        now = hist_ref[lag - 1]
        sum1 = sum1 + kr_ref[lag] * now + ki_ref[lag] * exchange(now)
        if lag >= 2:
            now = hist_ref[lag - 2]
            sum2 = sum2 + kr_ref[lag] * now + ki_ref[lag] * exchange(now)
    sum1s = exchange(sum1)

    def quarters(a, b, c, d):
        return jnp.where(
            lane8 < 32, a, jnp.where(lane8 < 64, b, jnp.where(lane8 < 96, c, d))
        )

    own = pl.ds(pl.multiple_of(me * cells, cells), cells)
    loads[0].wait()
    gather1[own, 128:256] = quarters(kr_ref[0], ki_ref[0], kr_ref[1], ki_ref[1])
    gather1[own, 0:128] = quarters(slip_tile(u1), sum1, sum1s, sum2)
    loads[1].wait()
    loads[2].wait()

    pl.semaphore_wait(barrier, n - 1)

    def to(device, source, target, index):
        return pltpu.make_async_remote_copy(
            src_ref=source, dst_ref=target, send_sem=halo_send.at[index],
            recv_sem=halo_recv.at[index], device_id=(group, device), device_id_type=MESH,
        )

    first = [
        to(left, u1.at[:, :, 1], u1.at[:, :, cells + 1], 0),
        to(right, u1.at[:, :, cells], u1.at[:, :, 0], 1),
        to(left, d1.at[:, 1], d1.at[:, cells + 1], 2),
        to(right, d1.at[:, cells], d1.at[:, 0], 3),
        to(left, face.at[:, 1], face.at[:, cells + 1], 4),
        to(right, face.at[:, cells], face.at[:, 0], 5),
    ]
    for copy in first:
        copy.start()

    def spread(buffer, index):
        @pl.loop(1, n)
        def _(step):
            pltpu.make_async_remote_copy(
                src_ref=buffer.at[own], dst_ref=buffer.at[own],
                send_sem=all_send.at[index], recv_sem=all_recv.at[index],
                device_id=(group, lax.rem(me + step, n)), device_id_type=MESH,
            ).start()

    def all_of(buffer, index):
        rest = buffer.at[pl.ds(0, (n - 1) * cells)]
        return pltpu.make_async_remote_copy(
            src_ref=rest, dst_ref=rest,
            send_sem=all_send.at[index], recv_sem=all_recv.at[index],
            device_id=(group, left), device_id_type=MESH,
        )

    spread(gather1, 0)

    zi = lax.broadcasted_iota(jnp.int32, (depth, rows), 0)
    yi = lax.broadcasted_iota(jnp.int32, (depth, rows), 1)
    ends = ((0, zi == depth - 1, depth - 1), (0, zi == 0, 1), (1, yi == rows - 1, rows - 1), (1, yi == 0, 1))

    def plane(u, d, s, x):
        here = d[s, x + 1]
        around = [d[s, x + 2], d[s, x]]
        for axis, at_end, shift in ends:
            around.append(jnp.where(at_end, here, pltpu.roll(here, shift, axis)))
        stiff = [1.0 - 0.5 * (here + other) for other in around]
        energy = None
        forces = []
        for c in range(2):
            mid = u[c, s, x + 1]
            near = [u[c, s, x + 2], u[c, s, x]]
            for axis, at_end, shift in ends:
                near.append(jnp.where(at_end, 0.0, pltpu.roll(mid, shift, axis)))
            force = stiff[0] * (near[0] - mid)
            for k in range(1, 6):
                force = force + stiff[k] * (near[k] - mid)
            forces.append(force)
            for k in range(3):
                slope = near[2 * k] - near[2 * k + 1]
                energy = slope * slope if energy is None else energy + slope * slope
        material = mat_ref[s, x]
        over = 0.25 * energy - class_lookup(material, table_ref, 1)
        soft = jnp.maximum(over, 0.0) + jnp.log(1.0 + jnp.exp(-jnp.abs(over)))
        kept = (1.0 - here) * jnp.exp(-class_lookup(material, table_ref, 0) * soft)
        return forces, 1.0 - kept

    def first_step(s, x):
        forces, damaged = plane(u1, d1, s, x)
        for c in range(2):
            speed = vel[c, s, x] + dt * forces[c]
            vel[c, s, x] = speed
            u2[c, s, x + 1] = u1[c, s, x + 1] + dt * speed
        d2[s, x + 1] = damaged

    @pl.loop(1, cells - 1)
    def _(x):
        for s in range(2):
            first_step(s, x)

    for copy in first:
        copy.wait_recv()

    @pl.loop(0, 2)
    def _(side):
        for s in range(2):
            first_step(s, side * (cells - 1))

    second = [
        to(left, u2.at[:, :, 1], u2.at[:, :, cells + 1], 6),
        to(right, u2.at[:, :, cells], u2.at[:, :, 0], 7),
        to(left, d2.at[:, 1], d2.at[:, cells + 1], 8),
        to(right, d2.at[:, cells], d2.at[:, 0], 9),
    ]
    gather2[own, :] = slip_tile(u2)
    spread(gather2, 1)
    for copy in second:
        copy.start()

    all_of(gather1, 0).wait_recv()
    waves = forward_ref.shape[0] // 2
    terms = gather1[:, 0:128]
    kernels = gather1[:, 128:256]
    spec1 = jnp.dot(forward_ref[...], terms, precision=HIGHEST, preferred_element_type=jnp.float32)
    cur, cur_s = spec1[:waves], spec1[waves:]
    kr0, ki0 = kernels, pltpu.roll(kernels, 96, 1)
    kr1, ki1 = pltpu.roll(kernels, 64, 1), pltpu.roll(kernels, 32, 1)
    tract1 = kr0 * cur + ki0 * cur_s + pltpu.roll(terms, 96, 1)
    tract1_s = kr0 * cur_s - ki0 * cur + pltpu.roll(terms, 64, 1)
    row = lax.broadcasted_iota(jnp.int32, (waves, 128), 0)
    wide = lax.broadcasted_iota(jnp.int32, (waves, 128), 1)
    back1 = 2.0 * dt * dt * jnp.where(row == 1, 0.0, tract1)
    back1_s = 2.0 * dt * dt * jnp.where(row == 0, 0.0, tract1_s)
    partial2 = kr1 * cur + ki1 * cur_s + pltpu.roll(terms, 32, 1)
    spectra[0] = cur

    all_of(gather2, 1).wait_recv()
    spec2 = jnp.dot(
        forward_ref[...], gather2[...], precision=HIGHEST, preferred_element_type=jnp.float32
    )
    cur2 = spec2[:waves] - back1
    cur2_s = spec2[waves:] - back1_s
    spectra[1] = cur2
    tract2 = kr0 * cur2 + ki0 * cur2_s + partial2
    both = jnp.where(wide < 32, tract1, jnp.where(wide < 64, pltpu.roll(tract2, 32, 1), 0.0))
    local = inverse_ref[pl.ds(pl.multiple_of(me * cells, cells), 3 * cells), :]
    traction = lax.dot_general(
        both.T, local, (((1,), (1,)), ((), ())), precision=HIGHEST,
        preferred_element_type=jnp.float32,
    )

    hist_out[0] = spectra[1, own, :]
    hist_out[1] = spectra[0, own, :]
    for lag in range(2, lags - 1):
        hist_out[lag] = hist_ref[lag - 2]

    for copy in second:
        copy.wait_recv()
        copy.wait_send()

    for x in range(cells + 2):
        for c in range(2):
            column = traction[c * depth : (c + 1) * depth, cells - 1 + x : cells + x]
            wide_column = jnp.broadcast_to(column, (depth, 128))
            for s, sign in ((0, dt), (1, -dt)):
                push = jnp.where(lane_f == face[s, x], sign * wide_column, 0.0)
                u2[c, s, x, :, :128] = u2[c, s, x, :, :128] + dt * push
                if 1 <= x <= cells:
                    vel[c, s, x - 1, :, :128] = vel[c, s, x - 1, :, :128] + push
            if 1 <= x <= cells:
                column = traction[(2 + c) * depth : (3 + c) * depth, cells - 1 + x : cells + x]
                push2[c, x - 1] = jnp.broadcast_to(dt * column, (depth, 128))

    @pl.loop(0, cells)
    def _(x):
        for s in range(2):
            forces, damaged = plane(u2, d2, s, x)
            on = lane_f == face[s, x + 1]
            for c in range(2):
                speed = vel[c, s, x] + dt * forces[c]
                push = jnp.where(on, push2[c, x], 0.0)
                near = speed[:, :128] + push if s == 0 else speed[:, :128] - push
                speed = jnp.concatenate([near, speed[:, 128:]], 1)
                vel_out[c, s, x] = speed
                disp_out[c, s, x] = u2[c, s, x + 1] + dt * speed
            dmg_out[s, x] = damaged

    for copy in first:
        copy.wait_send()
    all_of(gather1, 0).wait_send()
    all_of(gather2, 1).wait_send()


def per_device(displacement, velocity, damage, material, damage_table, fault_rows, kernel, history):
    n = lax.axis_size("long")
    parts, strips, cells, depth, rows = displacement.shape
    length = cells * n
    lags, owned = kernel.shape[0], kernel.shape[1]
    forward, inverse = bases(length, cells)

    def expanded(part):
        shape = (lags, owned, 2, 4, parts, depth)
        return jnp.broadcast_to(part[:, :, :, None, :, None], shape).reshape(lags, 2 * owned, 128)

    kr = expanded(jnp.stack([kernel[:, :, 0], kernel[:, :, 0]], 2))
    ki = expanded(jnp.stack([-kernel[:, :, 1], kernel[:, :, 1]], 2))
    hist = jnp.broadcast_to(
        history[:, :, :, None], (lags - 1, owned, 2, 4, parts, depth)
    ).reshape(lags - 1, 2 * owned, 128)
    f32 = jnp.float32
    vmem = pl.BlockSpec(memory_space=pltpu.VMEM)
    hbm = pl.BlockSpec(memory_space=pl.ANY)
    smem = pl.BlockSpec(memory_space=pltpu.SMEM)
    out = pl.pallas_call(
        functools.partial(body, n),
        out_shape=(
            jax.ShapeDtypeStruct(displacement.shape, f32),
            jax.ShapeDtypeStruct(velocity.shape, f32),
            jax.ShapeDtypeStruct(damage.shape, f32),
            jax.ShapeDtypeStruct(hist.shape, f32),
        ),
        in_specs=[hbm, hbm, hbm, vmem, smem, vmem, vmem, vmem, vmem, vmem, vmem],
        out_specs=(vmem, vmem, vmem, vmem),
        scratch_shapes=[
            pltpu.VMEM((parts, strips, cells + 2, depth, rows), f32),
            pltpu.VMEM((parts, strips, cells + 2, depth, rows), f32),
            pltpu.VMEM((strips, cells + 2, depth, rows), f32),
            pltpu.VMEM((strips, cells + 2, depth, rows), f32),
            pltpu.VMEM(velocity.shape, f32),
            pltpu.VMEM((strips, cells + 2, depth, 128), f32),
            pltpu.VMEM((length, 256), f32),
            pltpu.VMEM((length, 128), f32),
            pltpu.VMEM((2, length, 128), f32),
            pltpu.VMEM((parts, cells, depth, 128), f32),
            pltpu.SemaphoreType.DMA((3,)),
            pltpu.SemaphoreType.DMA((10,)),
            pltpu.SemaphoreType.DMA((10,)),
            pltpu.SemaphoreType.DMA((2,)),
            pltpu.SemaphoreType.DMA((2,)),
        ],
        compiler_params=pltpu.CompilerParams(
            collective_id=0, has_side_effects=True, vmem_limit_bytes=48 * 1024 * 1024
        ),
    )(
        displacement, velocity, damage, material, damage_table, fault_rows, kr, ki, hist,
        jnp.asarray(forward), jnp.asarray(inverse),
    )
    hist_new = out[3][:, :, : parts * depth].reshape(history.shape)
    return out[0], out[1], out[2], hist_new


def solution(mesh):
    placed = (
        P("groups", None, "long", None, None),
        P("groups", None, "long", None, None),
        P("groups", "long", None, None),
        P("groups", "long", None, None),
        P(),
        P("groups", "long", None),
        P(None, "long", None, None),
        P("groups", "long", None, None, None),
    )
    return jax.shard_map(
        per_device,
        mesh=mesh,
        in_specs=placed,
        out_specs=(
            P("groups", None, "long", None, None),
            P("groups", None, "long", None, None),
            P("groups", "long", None, None),
            P("groups", "long", None, None, None),
        ),
        check_vma=False,
    )
```

time: 215 us -> 27.1 us (0.13)
  blocking collectives: 161 us -> 0 us
  other arithmetic: 29.3 us -> 0.72 us
  Pallas kernels: 0 us -> 19.1 us
  starting transfers between devices: 10.1 us -> 0 us
  matrix products: 3.4 us -> 0 us
    unnamed x2 -> x0, blocking collectives: 126 us -> none
    all_gather x2 -> x0, blocking collectives: 35 us -> none  [per_device(): lax.all_gather(traction_spectrum, 'long', axis=0, tiled=True)]
    pallas_call x0 -> x1, Pallas kernels: none -> 19.1 us  [per_device(): pl.pallas_call(functools.partial(body, n), out_shape=(jax.ShapeDtypeStruc...]
    sub x2 -> x0, other arithmetic: 12.3 us -> none  [the longest x1 6.16 us: advance(): 1.0 - (1.0 - dmg_mid) * jnp.exp(-rate_mid * jax.nn.softplus(energy - limi...]
    ppermute x4 -> x0, starting transfers between devices: 10.1 us -> none  [the longest x2 9.16 us: padded_2(): lax.ppermute(lax.slice_in_dim(block, 0, width, axis=dim), axis, backward)]
    mul x7 -> x0, other arithmetic: 4.95 us -> none  [the longest x2 2.76 us: local_terms(): forces = forces + (0.5 * (centre_c + above_c))[None] * (above_u - centre_u)]
    reduce_sum x5 -> x0, other arithmetic: 3.91 us -> none  [the longest x3 3.48 us: local_terms(): energy = energy + jnp.sum(gradient * gradient, axis=0)]
    slice x10 -> x0, local copies, waits for them, and re-layouts: 3.72 us -> none  [the longest x4 1.68 us: local_terms(): outer_c = jnp.pad(padded_c, ((0, 0), (0, 0), (1, 1), (1, 1)), mode='edge')]
  transfers between devices with their start and end apart: 4 -> 0, of which waited for: 1 -> 0; matrix products, arithmetic and copies ran while one was open for 1% -> 0% of each run, Pallas kernels for 0% -> 0%
where the time goes in v1:
time: 27.1 us; the launch traced here: 26.9 us
  Pallas kernels  19.1 us (70%)
  local copies, waits for them, and re-layouts  6.27 us (23%)
  between operations  0.76 us (3%)
  other arithmetic  0.72 us (3%)
    pallas_call x1, Pallas kernels, per_device(): pl.pallas_call(functools.partial(body, n), out_shape=(jax.ShapeDtypeStruc...  19.1 us
    unnamed x21, local copies, waits for them, and re-layouts  2.79 us
    reshape x2, local copies, waits for them, and re-layouts, expanded(): jnp.broadcast_to(part[:, :, :, None, :, None], shape)  1.3 us
    reshape x1, local copies, waits for them, and re-layouts, per_device(): hist_new = out[3][:, :, :parts * depth].reshape(history.shape)  0.78 us
    neg x1, other arithmetic, per_device(): ki = expanded(jnp.stack([-kernel[:, :, 1], kernel[:, :, 1]], 2))  0.71 us
    reshape x1, local copies, waits for them, and re-layouts, per_device(): hist = jnp.broadcast_to(history[:, :, :, None], (lags - 1, owned, 2, 4, p...  0.6 us

profile of v1, /device:TPU:0, one launch (start us, length us, event | category | flops | bytes accessed | tf_op | source)
XLA Modules:
  0.0 26.9 jit_solution(8265735277464955079)
XLA Ops:
  0.6 0.7 %slice_negate_fusion = (f32[16,4,1,2]{0,3,2,1:T(2,128)S(1)}, f32[16,4,1,2]{0,3,2,1:T(2,128)S(1)}, f32[16,4,1,2]{0,3,2,1:T(2,128)S(1)}) fusion(f32[16,4,2,2]{0,3,2,1:T(2,128)} %param.16), kind=kLoop, calls=%fused_computation.2 | loop fusion | flops 128 | bytes 2560 | tf_op jit(solution)/shard_map/neg | solution.py:314
  1.4 0.1 copy.14
  1.5 0.2 broadcast_in_dim.6
  1.7 0.6 %reshape.23.kr_ref = f32[16,8,128]{2,1,0:T(8,128)S(1)} reshape(f32[16,4,2,4,2,16]{5,4,3,2,1,0:T(2,128)S(1)} %broadcast_in_dim.6) | data formatting | bytes 131072 | tf_op jit(solution)/shard_map/reshape | solution.py:311
  2.3 0.1 copy.15
  2.5 0.0 copy-start.8
  2.5 0.0 copy-start.5
  2.5 0.2 broadcast_in_dim.7
  2.7 0.0 copy-start.2
  2.7 0.0 copy-start.3
  2.7 0.0 copy-start.4
  2.8 0.7 %reshape.24.ki_ref = f32[16,8,128]{2,1,0:T(8,128)S(1)} reshape(f32[16,4,2,4,2,16]{5,4,3,2,1,0:T(2,128)S(1)} %broadcast_in_dim.7) | data formatting | bytes 131072 | tf_op jit(solution)/shard_map/reshape | solution.py:311
  3.4 0.0 copy-start.1
  3.4 0.1 broadcast_in_dim.8
  3.6 0.0 copy-start.6
  3.6 0.0 copy-start.7
  3.6 0.6 %reshape.25.hist_ref = f32[15,8,128]{2,1,0:T(8,128)S(1)} reshape(f32[15,4,2,4,2,16]{5,4,3,2,1,0:T(2,128)S(1)} %broadcast_in_dim.8) | data formatting | bytes 122880 | tf_op jit(solution)/shard_map/reshape | solution.py:317
  4.2 0.3 %copy-done = f32[2,2,8,16,256]{4,3,2,1,0:T(8,128)S(1)} copy-done((f32[2,2,8,16,256]{4,3,2,1,0:T(8,128)S(1)}, f32[2,2,8,16,256]{4,3,2,1,0:T(8,128)}, u32[]{:S(2)}) %copy-start) | copy-done | bytes 524312
  4.5 0.2 copy-done.1
  4.7 19.1 %shard_map.129 = (f32[2,2,8,16,256]{4,3,2,1,0:T(8,128)S(1)}, f32[2,2,8,16,256]{4,3,2,1,0:T(8,128)S(1)}, f32[2,8,16,256]{3,2,1,0:T(8,128)S(1)}, f32[15,8,128]{2,1,0:T(8,128)S(1)}) custom-call(f32[2,2,8,16,256]{4,3,2,1,0:T(8,128)S(1)} %copy-done, f32[2,2,8,16,256]{4,3,2,1,0:T(8,128)S(1)} %copy-done.1, f32[2,8,16,256]{3,2,1,0:T(8,128)S(1)} %copy-done.2, ...), custom_call_target="tpu_custom_call" | custom-call | tf_op jit(solution)/shard_map/pallas_call | solution.py:322
  23.8 0.8 %reshape.26 = f32[15,4,2,2,16]{4,3,2,1,0:T(2,128)} reshape(f32[15,8,32]{2,1,0:T(8,128)S(1)} %bitcast.1) | data formatting | bytes 30720 | tf_op jit(solution)/shard_map/reshape | solution.py:356
  24.6 0.8 %copy.19 = f32[2,2,8,16,256]{4,3,2,1,0:T(8,128)} copy(f32[2,2,8,16,256]{4,3,2,1,0:T(8,128)S(1)} %get-tuple-element.21) | data formatting | bytes 1048576
  25.4 0.8 %copy.20 = f32[2,2,8,16,256]{4,3,2,1,0:T(8,128)} copy(f32[2,2,8,16,256]{4,3,2,1,0:T(8,128)S(1)} %get-tuple-element.22) | data formatting | bytes 1048576
  26.2 0.7 %copy.21 = f32[2,8,16,256]{3,2,1,0:T(8,128)} copy(f32[2,8,16,256]{3,2,1,0:T(8,128)S(1)} %get-tuple-element.23) | data formatting | bytes 524288
  (9 shorter events, 0.0 us)
Async XLA Ops:
  2.5 0.9 %copy-start.8 = (f32[15,4,2,2,16]{4,3,2,1,0:T(2,128)S(1)}, f32[15,4,2,2,16]{4,3,2,1,0:T(2,128)}, u32[]{:S(2)}) copy-start(f32[15,4,2,2,16]{4,3,2,1,0:T(2,128)} %param.17) | copy-start | bytes 46084
  2.5 1.7 %copy-start.5 = (f32[144,128]{1,0:T(8,128)S(1)}, f32[144,128]{1,0:T(8,128)}, u32[]{:S(2)}) copy-start(f32[144,128]{1,0:T(8,128)} %constant.5.clone.inverse_ref) | copy-start | bytes 221188
  2.7 1.5 %copy-start.2 = (f32[2,8,16,256]{3,2,1,0:T(8,128)S(1)}, f32[2,8,16,256]{3,2,1,0:T(8,128)}, u32[]{:S(2)}) copy-start(f32[2,8,16,256]{3,2,1,0:T(8,128)} %dmg_hbm.1) | copy-start | bytes 786436
  2.7 1.5 %copy-start.3 = (s32[2,8,16,256]{3,2,1,0:T(8,128)S(1)}, s32[2,8,16,256]{3,2,1,0:T(8,128)}, u32[]{:S(2)}) copy-start(s32[2,8,16,256]{3,2,1,0:T(8,128)} %mat_ref.1) | copy-start | bytes 786436
  2.7 1.5 %copy-start.4 = (f32[256,128]{1,0:T(8,128)S(1)}, f32[256,128]{1,0:T(8,128)}, u32[]{:S(2)}) copy-start(f32[256,128]{1,0:T(8,128)} %constant.4.clone.forward_ref) | copy-start | bytes 393220
  3.4 1.1 %copy-start = (f32[2,2,8,16,256]{4,3,2,1,0:T(8,128)S(1)}, f32[2,2,8,16,256]{4,3,2,1,0:T(8,128)}, u32[]{:S(2)}) copy-start(f32[2,2,8,16,256]{4,3,2,1,0:T(8,128)} %disp_hbm.1) | copy-start | bytes 1572868
  3.4 1.3 %copy-start.1 = (f32[2,2,8,16,256]{4,3,2,1,0:T(8,128)S(1)}, f32[2,2,8,16,256]{4,3,2,1,0:T(8,128)}, u32[]{:S(2)}) copy-start(f32[2,2,8,16,256]{4,3,2,1,0:T(8,128)} %vel_hbm.1) | copy-start | bytes 1572868
  3.6 1.1 %copy-start.6 = (s32[2,8,16]{2,1,0:T(8,128)S(1)}, s32[2,8,16]{2,1,0:T(8,128)}, u32[]{:S(2)}) copy-start(s32[2,8,16]{2,1,0:T(8,128)} %fault_ref.1) | copy-start | bytes 3076
  3.6 1.1 %copy-start.7 = (f32[2,4]{1,0:T(2,128)S(1)}, f32[2,4]{1,0:T(2,128)}, u32[]{:S(2)}) copy-start(f32[2,4]{1,0:T(2,128)} %table_ref.1) | copy-start | bytes 100

commit v2 on v1

v2 whole, which is shorter than its diff:
```python
import functools
import math

import jax
import jax.numpy as jnp
import numpy as np
from jax import lax
from jax.experimental import pallas as pl
from jax.experimental.pallas import tpu as pltpu
from jax.sharding import PartitionSpec as P

time_step = 0.5
MESH = pl.DeviceIdType.MESH
HIGHEST = lax.Precision.HIGHEST


def bases(length, cells):
    waves = np.arange(length // 2)
    places = np.arange(length)
    norming = 1.0 / math.sqrt(length)

    def table(k, x):
        phase = (k[:, None] * x[None, :] % length) * (2.0 * math.pi / length)
        return np.cos(phase) * norming, -np.sin(phase) * norming

    cosine, sine = table(waves, places)
    forward = np.stack([cosine, sine], 1).reshape(length, length)
    swapped = np.stack([sine, cosine], 1).reshape(length, length)
    cosine, sine = table(waves, np.arange(-cells, length + cells))
    weights = np.where(waves == 0, 1.0, 2.0)[:, None]
    inverse = np.stack([cosine * weights, sine * weights], 1).reshape(length, -1).T
    return np.concatenate([forward, swapped], 0).astype(np.float32), inverse.astype(np.float32)


def class_lookup(material, table_ref, row):
    count = table_ref.shape[1]
    result = jnp.full(material.shape, table_ref[row, count - 1])
    for level in range(count - 1):
        result = jnp.where(material == level, table_ref[row, level], result)
    return result


def half(lanes):
    return slice(128 * lanes, 128 * lanes + 128)


def plane(u, d, mat_ref, table_ref, s, x, h, depth):
    zi = lax.broadcasted_iota(jnp.int32, (depth, 128), 0)
    yi = lax.broadcasted_iota(jnp.int32, (depth, 128), 1)

    def nearby(ref, index, own_value, here):
        before, after = index
        near = [ref[(*after, slice(None), half(h))], ref[(*before, slice(None), half(h))]]
        end = here if own_value else 0.0
        near.append(jnp.where(zi == depth - 1, end, pltpu.roll(here, depth - 1, 0)))
        near.append(jnp.where(zi == 0, end, pltpu.roll(here, 1, 0)))
        middle = (*after[:-1], x + 1)
        other = ref[(*middle, slice(None), half(1 - h))]
        high, low = end, end
        if h == 0:
            high = pltpu.roll(other, 127, 1)
        else:
            low = pltpu.roll(other, 1, 1)
        near.append(jnp.where(yi == 127, high, pltpu.roll(here, 127, 1)))
        near.append(jnp.where(yi == 0, low, pltpu.roll(here, 1, 1)))
        return near

    here = d[s, x + 1, :, half(h)]
    stiff = [1.0 - 0.5 * (here + other) for other in nearby(d, ((s, x), (s, x + 2)), True, here)]
    energy = None
    forces = []
    for c in range(2):
        mid = u[c, s, x + 1, :, half(h)]
        near = nearby(u, ((c, s, x), (c, s, x + 2)), False, mid)
        force = stiff[0] * (near[0] - mid)
        for k in range(1, 6):
            force = force + stiff[k] * (near[k] - mid)
        forces.append(force)
        for k in range(3):
            slope = near[2 * k] - near[2 * k + 1]
            energy = slope * slope if energy is None else energy + slope * slope
    material = mat_ref[s, x, :, half(h)]
    over = 0.25 * energy - class_lookup(material, table_ref, 1)
    soft = jnp.maximum(over, 0.0) + jnp.log(1.0 + jnp.exp(-jnp.abs(over)))
    kept = (1.0 - here) * jnp.exp(-class_lookup(material, table_ref, 0) * soft)
    return forces, 1.0 - kept


def exchange_body(
    n, disp_hbm, vel_hbm, dmg_hbm, mat_ref, table_ref, fault_ref, kern_ref, hist_ref,
    forward_ref, inverse_ref,
    u2, d2, vel, face, push2, spec_out, disp_far, vel_far, dmg_far,
    u1, d1, gather1, gather2, spectra, small,
    load_sems, halo_send, halo_recv, all_send, all_recv,
):
    cells = vel.shape[2]
    depth = vel.shape[3]
    group = lax.axis_index("groups")
    me = lax.axis_index("long")
    left, right = lax.rem(me + n - 1, n), lax.rem(me + 1, n)
    dt = time_step

    barrier = pltpu.get_barrier_semaphore()

    @pl.loop(1, n)
    def _(step):
        pl.semaphore_signal(
            barrier, inc=1, device_id=(group, lax.rem(me + step, n)), device_id_type=MESH
        )

    loads = [
        pltpu.make_async_copy(disp_hbm, u1.at[:, :, pl.ds(1, cells)], load_sems.at[0]),
        pltpu.make_async_copy(dmg_hbm, d1.at[:, pl.ds(1, cells)], load_sems.at[1]),
        pltpu.make_async_copy(vel_hbm, vel, load_sems.at[2]),
    ]
    for copy in loads:
        copy.start()

    diagonal = lax.broadcasted_iota(jnp.int32, (depth, depth), 0) == lax.broadcasted_iota(
        jnp.int32, (depth, depth), 1
    )
    for s in range(2):
        rows_s = fault_ref[s].astype(jnp.float32)
        for x in range(cells):
            line = jnp.where(diagonal, rows_s[x : x + 1, :], 0.0)
            column = jnp.sum(line, axis=1, keepdims=True)
            face[s, x + 1] = jnp.broadcast_to(column, (depth, 128))

    lane = lax.broadcasted_iota(jnp.int32, (depth, 128), 1)
    lane_f = lane.astype(jnp.float32)
    lane8 = lax.broadcasted_iota(jnp.int32, (cells, 128), 1)

    def slip_tile(u):
        parts = []
        for c in range(2):
            total = jnp.zeros((depth, 128), jnp.float32)
            for x in range(cells):
                on0 = jnp.where(lane_f == face[0, x + 1], u[c, 0, x + 1, :, :128], 0.0)
                on1 = jnp.where(lane_f == face[1, x + 1], u[c, 1, x + 1, :, :128], 0.0)
                column = jnp.sum(on1 - on0, axis=1, keepdims=True)
                total = jnp.where(lane == x, column, total)
            parts.append(total)
        parts.append(jnp.zeros((128 - 2 * depth, 128), jnp.float32))
        return jnp.concatenate(parts, 0).T[:cells, :]

    odd = lax.broadcasted_iota(jnp.int32, (cells, 128), 0) % 2 == 1

    def exchange(block):
        return jnp.where(odd, pltpu.roll(block, 1, 0), pltpu.roll(block, cells - 1, 0))

    owned, lags = kern_ref.shape[0], kern_ref.shape[3]
    real, imag = kern_ref[:, 0], kern_ref[:, 1]
    at_lag = [
        [jnp.broadcast_to(part[:, :, lag : lag + 1], (owned, 2, depth)) for part in (real, imag)]
        for lag in range(lags)
    ]
    zero = jnp.zeros((owned, 2, depth), jnp.float32)
    sums = [[zero, zero], [zero, zero]]
    for lag in range(1, lags):
        kr, ki = at_lag[lag]
        for step in range(2):
            if lag - 1 - step >= 0:
                now_r, now_i = hist_ref[lag - 1 - step, :, 0], hist_ref[lag - 1 - step, :, 1]
                old_r, old_i = sums[step]
                sums[step] = [old_r + kr * now_r - ki * now_i, old_i + kr * now_i + ki * now_r]
    pairs = [
        (at_lag[0][0], at_lag[0][0]), (-at_lag[0][1], at_lag[0][1]),
        (at_lag[1][0], at_lag[1][0]), (-at_lag[1][1], at_lag[1][1]),
        sums[0], sums[1],
    ]
    small[...] = jnp.zeros_like(small)
    for q, pair in enumerate(pairs):
        for ri in range(2):
            for k in range(owned):
                for c in range(2):
                    at = c * cells + 2 * k + ri
                    small[q, at : at + 1, 0:depth] = pair[ri][k, c : c + 1, :]

    def packed(q):
        second = pltpu.roll(small[q, cells : 2 * cells], depth, 1)
        return jnp.where(lane8 < depth, small[q, 0:cells], second)

    def quarters(parts):
        a, b, c, d = [p if i == 0 else pltpu.roll(p, 32 * i, 1) for i, p in enumerate(parts)]
        return jnp.where(
            lane8 < 32, a, jnp.where(lane8 < 64, b, jnp.where(lane8 < 96, c, d))
        )

    own = pl.ds(pl.multiple_of(me * cells, cells), cells)
    gather1[own, 128:256] = quarters([packed(q) for q in range(4)])
    sum1 = packed(4)
    loads[0].wait()
    gather1[own, 0:128] = quarters([slip_tile(u1), sum1, exchange(sum1), packed(5)])
    loads[1].wait()
    loads[2].wait()

    pl.semaphore_wait(barrier, n - 1)

    def to(device, source, target, index):
        return pltpu.make_async_remote_copy(
            src_ref=source, dst_ref=target, send_sem=halo_send.at[index],
            recv_sem=halo_recv.at[index], device_id=(group, device), device_id_type=MESH,
        )

    def halo(u, d, h, index):
        lanes = pl.ds(128 * h, 128)
        everything = slice(None)
        return [
            to(left, u.at[:, :, 1, everything, lanes], u.at[:, :, cells + 1, everything, lanes], index),
            to(right, u.at[:, :, cells, everything, lanes], u.at[:, :, 0, everything, lanes], index + 1),
            to(left, d.at[:, 1, everything, lanes], d.at[:, cells + 1, everything, lanes], index + 2),
            to(right, d.at[:, cells, everything, lanes], d.at[:, 0, everything, lanes], index + 3),
        ]

    def spread(buffer, index):
        @pl.loop(1, n)
        def _(step):
            pltpu.make_async_remote_copy(
                src_ref=buffer.at[own], dst_ref=buffer.at[own],
                send_sem=all_send.at[index], recv_sem=all_recv.at[index],
                device_id=(group, lax.rem(me + step, n)), device_id_type=MESH,
            ).start()

    def all_of(buffer, index):
        rest = buffer.at[pl.ds(0, (n - 1) * cells)]
        return pltpu.make_async_remote_copy(
            src_ref=rest, dst_ref=rest,
            send_sem=all_send.at[index], recv_sem=all_recv.at[index],
            device_id=(group, left), device_id_type=MESH,
        )

    faces = [
        to(left, face.at[:, 1], face.at[:, cells + 1], 16),
        to(right, face.at[:, cells], face.at[:, 0], 17),
    ]
    near1 = halo(u1, d1, 0, 0)
    far1 = halo(u1, d1, 1, 4)
    for copy in near1:
        copy.start()
    spread(gather1, 0)
    for copy in far1 + faces:
        copy.start()

    def first_step(s, x, h):
        forces, damaged = plane(u1, d1, mat_ref, table_ref, s, x, h, depth)
        for c in range(2):
            speed = vel[c, s, x, :, half(h)] + dt * forces[c]
            vel[c, s, x, :, half(h)] = speed
            u2[c, s, x + 1, :, half(h)] = u1[c, s, x + 1, :, half(h)] + dt * speed
        d2[s, x + 1, :, half(h)] = damaged

    def step_half(h, arrivals):
        @pl.loop(1, cells - 1)
        def _(x):
            for s in range(2):
                first_step(s, x, h)

        for copy in arrivals:
            copy.wait_recv()

        @pl.loop(0, 2)
        def _(side):
            for s in range(2):
                first_step(s, side * (cells - 1), h)

    step_half(0, near1)
    gather2[own, :] = slip_tile(u2)
    spread(gather2, 1)
    near2 = halo(u2, d2, 0, 8)
    for copy in near2:
        copy.start()
    step_half(1, far1)
    far2 = halo(u2, d2, 1, 12)
    for copy in far2:
        copy.start()

    all_of(gather1, 0).wait_recv()
    waves = forward_ref.shape[0] // 2
    terms = gather1[:, 0:128]
    kernels = gather1[:, 128:256]
    spec1 = jnp.dot(forward_ref[...], terms, precision=HIGHEST, preferred_element_type=jnp.float32)
    cur, cur_s = spec1[:waves], spec1[waves:]
    kr0, ki0 = kernels, pltpu.roll(kernels, 96, 1)
    kr1, ki1 = pltpu.roll(kernels, 64, 1), pltpu.roll(kernels, 32, 1)
    tract1 = kr0 * cur + ki0 * cur_s + pltpu.roll(terms, 96, 1)
    tract1_s = kr0 * cur_s - ki0 * cur + pltpu.roll(terms, 64, 1)
    row = lax.broadcasted_iota(jnp.int32, (waves, 128), 0)
    wide = lax.broadcasted_iota(jnp.int32, (waves, 128), 1)
    back1 = 2.0 * dt * dt * jnp.where(row == 1, 0.0, tract1)
    back1_s = 2.0 * dt * dt * jnp.where(row == 0, 0.0, tract1_s)
    partial2 = kr1 * cur + ki1 * cur_s + pltpu.roll(terms, 32, 1)
    spectra[0] = cur

    for copy in near2 + far2:
        copy.wait_recv()
        copy.wait_send()

    @pl.loop(0, cells)
    def _(x):
        for s in range(2):
            forces, damaged = plane(u2, d2, mat_ref, table_ref, s, x, 1, depth)
            for c in range(2):
                speed = vel[c, s, x, :, half(1)] + dt * forces[c]
                vel_far[c, s, x] = speed
                disp_far[c, s, x] = u2[c, s, x + 1, :, half(1)] + dt * speed
            dmg_far[s, x] = damaged

    all_of(gather2, 1).wait_recv()
    spec2 = jnp.dot(
        forward_ref[...], gather2[...], precision=HIGHEST, preferred_element_type=jnp.float32
    )
    cur2 = spec2[:waves] - back1
    cur2_s = spec2[waves:] - back1_s
    spectra[1] = cur2
    tract2 = kr0 * cur2 + ki0 * cur2_s + partial2
    both = jnp.where(wide < 32, tract1, jnp.where(wide < 64, pltpu.roll(tract2, 32, 1), 0.0))
    local = inverse_ref[pl.ds(pl.multiple_of(me * cells, cells), 3 * cells), :]
    traction = lax.dot_general(
        both.T, local, (((1,), (1,)), ((), ())), precision=HIGHEST,
        preferred_element_type=jnp.float32,
    )
    spec_out[0] = spectra[1, own, :]
    spec_out[1] = spectra[0, own, :]

    for copy in faces:
        copy.wait_recv()
    for copy in faces + near1 + far1:
        copy.wait_send()

    for x in range(cells + 2):
        for c in range(2):
            column = traction[c * depth : (c + 1) * depth, cells - 1 + x : cells + x]
            wide_column = jnp.broadcast_to(column, (depth, 128))
            for s, sign in ((0, dt), (1, -dt)):
                push = jnp.where(lane_f == face[s, x], sign * wide_column, 0.0)
                u2[c, s, x, :, :128] = u2[c, s, x, :, :128] + dt * push
                if 1 <= x <= cells:
                    vel[c, s, x - 1, :, :128] = vel[c, s, x - 1, :, :128] + push
            if 1 <= x <= cells:
                column = traction[(2 + c) * depth : (3 + c) * depth, cells - 1 + x : cells + x]
                push2[c, x - 1] = jnp.broadcast_to(dt * column, (depth, 128))

    all_of(gather1, 0).wait_send()
    all_of(gather2, 1).wait_send()


def finish_body(
    u2, d2, vel, face, push2, spec, disp_far, vel_far, dmg_far, mat_ref, table_ref, hist_hbm,
    disp_out, vel_out, dmg_out, hist_out,
    disp_near, vel_near, dmg_near, newest, sems,
):
    cells, depth = vel.shape[2], vel.shape[3]
    owned = newest.shape[1]
    kept = hist_hbm.shape[0] - 2
    dt = time_step
    far = pl.ds(128, 128)
    near = pl.ds(0, 128)
    everything = slice(None)
    moves = [
        pltpu.make_async_copy(hist_hbm.at[pl.ds(0, kept)], hist_out.at[pl.ds(2, kept)], sems.at[0]),
        pltpu.make_async_copy(disp_far, disp_out.at[:, :, :, everything, far], sems.at[1]),
        pltpu.make_async_copy(vel_far, vel_out.at[:, :, :, everything, far], sems.at[2]),
        pltpu.make_async_copy(dmg_far, dmg_out.at[:, :, everything, far], sems.at[3]),
    ]
    for copy in moves:
        copy.start()
    for step in range(2):
        lines = spec[step]
        shifted = pltpu.roll(lines, 128 - depth, 1)
        for k in range(owned):
            for ri in range(2):
                at = 2 * k + ri
                newest[step, k, ri, 0:1, :] = lines[at : at + 1, 0:depth]
                newest[step, k, ri, 1:2, :] = shifted[at : at + 1, 0:depth]
    last = pltpu.make_async_copy(newest, hist_out.at[pl.ds(0, 2)], sems.at[4])
    last.start()
    lane_f = lax.broadcasted_iota(jnp.int32, (depth, 128), 1).astype(jnp.float32)

    @pl.loop(0, cells)
    def _(x):
        for s in range(2):
            forces, damaged = plane(u2, d2, mat_ref, table_ref, s, x, 0, depth)
            on = lane_f == face[s, x + 1]
            for c in range(2):
                push = jnp.where(on, push2[c, x], 0.0)
                speed = vel[c, s, x, :, half(0)] + dt * forces[c]
                speed = speed + push if s == 0 else speed - push
                vel_near[c, s, x] = speed
                disp_near[c, s, x] = u2[c, s, x + 1, :, half(0)] + dt * speed
            dmg_near[s, x] = damaged
        pltpu.make_async_copy(
            disp_near.at[:, :, x], disp_out.at[:, :, x, everything, near], sems.at[5]
        ).start()
        pltpu.make_async_copy(
            vel_near.at[:, :, x], vel_out.at[:, :, x, everything, near], sems.at[6]
        ).start()
        pltpu.make_async_copy(
            dmg_near.at[:, x], dmg_out.at[:, x, everything, near], sems.at[7]
        ).start()

    for copy in moves:
        copy.wait()
    last.wait()
    pltpu.make_async_copy(disp_near, disp_out.at[:, :, :, everything, near], sems.at[5]).wait()
    pltpu.make_async_copy(vel_near, vel_out.at[:, :, :, everything, near], sems.at[6]).wait()
    pltpu.make_async_copy(dmg_near, dmg_out.at[:, :, everything, near], sems.at[7]).wait()


def per_device(displacement, velocity, damage, material, damage_table, fault_rows, kernel, history):
    n = lax.axis_size("long")
    parts, strips, cells, depth, rows = displacement.shape
    length = cells * n
    owned = kernel.shape[1]
    forward, inverse = bases(length, cells)
    f32 = jnp.float32
    vmem = pl.BlockSpec(memory_space=pltpu.VMEM)
    hbm = pl.BlockSpec(memory_space=pltpu.HBM)
    smem = pl.BlockSpec(memory_space=pltpu.SMEM)
    narrow = (depth, 128)
    kern = jnp.transpose(kernel, (1, 2, 3, 0))
    middle = pl.pallas_call(
        functools.partial(exchange_body, n),
        out_shape=[
            jax.ShapeDtypeStruct(shape, f32)
            for shape in (
                (parts, strips, cells + 2, depth, rows),
                (strips, cells + 2, depth, rows),
                velocity.shape,
                (strips, cells + 2, *narrow),
                (parts, cells, *narrow),
                (2, cells, 128),
                (parts, strips, cells, *narrow),
                (parts, strips, cells, *narrow),
                (strips, cells, *narrow),
            )
        ],
        in_specs=[hbm, hbm, hbm, vmem, smem, vmem, vmem, vmem, vmem, vmem],
        out_specs=[vmem] * 9,
        scratch_shapes=[
            pltpu.VMEM((parts, strips, cells + 2, depth, rows), f32),
            pltpu.VMEM((strips, cells + 2, depth, rows), f32),
            pltpu.VMEM((length, 256), f32),
            pltpu.VMEM((length, 128), f32),
            pltpu.VMEM((2, length, 128), f32),
            pltpu.VMEM((6, 2 * cells, 128), f32),
            pltpu.SemaphoreType.DMA((3,)),
            pltpu.SemaphoreType.DMA((18,)),
            pltpu.SemaphoreType.DMA((18,)),
            pltpu.SemaphoreType.DMA((2,)),
            pltpu.SemaphoreType.DMA((2,)),
        ],
        compiler_params=pltpu.CompilerParams(
            collective_id=0, has_side_effects=True, vmem_limit_bytes=40 * 1024 * 1024
        ),
    )(
        displacement, velocity, damage, material, damage_table, fault_rows, kern, history,
        jnp.asarray(forward), jnp.asarray(inverse),
    )
    return pl.pallas_call(
        finish_body,
        out_shape=tuple(
            jax.ShapeDtypeStruct(a.shape, f32) for a in (displacement, velocity, damage, history)
        ),
        in_specs=[vmem] * 10 + [smem, hbm],
        out_specs=(hbm, hbm, hbm, hbm),
        scratch_shapes=[
            pltpu.VMEM((parts, strips, cells, *narrow), f32),
            pltpu.VMEM((parts, strips, cells, *narrow), f32),
            pltpu.VMEM((strips, cells, *narrow), f32),
            pltpu.VMEM((2, owned, 2, parts, depth), f32),
            pltpu.SemaphoreType.DMA((8,)),
        ],
        compiler_params=pltpu.CompilerParams(vmem_limit_bytes=24 * 1024 * 1024),
    )(*middle, material, damage_table, history)


def solution(mesh):
    placed = (
        P("groups", None, "long", None, None),
        P("groups", None, "long", None, None),
        P("groups", "long", None, None),
        P("groups", "long", None, None),
        P(),
        P("groups", "long", None),
        P(None, "long", None, None),
        P("groups", "long", None, None, None),
    )
    return jax.shard_map(
        per_device,
        mesh=mesh,
        in_specs=placed,
        out_specs=(
            P("groups", None, "long", None, None),
            P("groups", None, "long", None, None),
            P("groups", "long", None, None),
            P("groups", "long", None, None, None),
        ),
        check_vma=False,
    )
```

time: 27.1 us -> 31.6 us (1.17)
  Pallas kernels: 19.1 us -> 21.8 us
  local copies, waits for them, and re-layouts: 6.27 us -> 8.73 us
  other arithmetic: 0.72 us -> 0 us
    unnamed x21 -> x20, local copies, waits for them, and re-layouts: 2.79 us -> 8.73 us
    reshape x4 -> x0, local copies, waits for them, and re-layouts: 2.68 us -> none  [the longest x2 1.3 us: expanded(): jnp.broadcast_to(part[:, :, :, None, :, None], shape)]
    pallas_call x1 -> x2, Pallas kernels: 19.1 us -> 21.8 us  [the longest x1 19.4 us: per_device(): pl.pallas_call(functools.partial(exchange_body, n), out_shape=[jax.ShapeD...]
    neg x1 -> x0, other arithmetic: 0.71 us -> none  [per_device(): ki = expanded(jnp.stack([-kernel[:, :, 1], kernel[:, :, 1]], 2))]
    broadcast_in_dim x3 -> x0, local copies, waits for them, and re-layouts: 0.53 us -> none  [the longest x2 0.4 us: expanded(): jnp.broadcast_to(part[:, :, :, None, :, None], shape)]
where the time goes in v2:
time: 31.6 us; the launch traced here: 31.2 us
  Pallas kernels  21.8 us (69%)
  local copies, waits for them, and re-layouts  8.73 us (28%)
  between operations  0.66 us (2%)
    pallas_call x1, Pallas kernels, per_device(): pl.pallas_call(functools.partial(exchange_body, n), out_shape=[jax.ShapeD...  19.4 us
    unnamed x20, local copies, waits for them, and re-layouts  8.73 us
    pallas_call x1, Pallas kernels, per_device(): pl.pallas_call(finish_body, out_shape=tuple((jax.ShapeDtypeStruct(a.shape...  2.4 us

profile of v2, /device:TPU:0, one launch (start us, length us, event | category | flops | bytes accessed | tf_op | source)
XLA Modules:
  0.0 31.2 jit_solution(15410560247292498546)
XLA Ops:
  0.6 0.0 copy-start.9
  0.6 0.7 %copy-done.9 = f32[2,4]{1,0:T(2,128)S(1)} copy-done((f32[2,4]{1,0:T(2,128)S(1)}, f32[2,4]{1,0:T(2,128)}, u32[]{:S(2)}) %copy-start.9) | copy-done | bytes 56
  1.3 0.0 copy-start
  1.3 0.9 %copy-done = s32[2,8,16,256]{3,2,1,0:T(8,128)S(1)} copy-done((s32[2,8,16,256]{3,2,1,0:T(8,128)S(1)}, s32[2,8,16,256]{3,2,1,0:T(8,128)}, u32[]{:S(2)}) %copy-start) | copy-done | bytes 262168
  2.3 0.0 copy-start.1
  2.3 1.0 %copy-done.1 = f32[2,2,8,16,256]{4,3,2,1,0:T(8,128)S(1)} copy-done((f32[2,2,8,16,256]{4,3,2,1,0:T(8,128)S(1)}, f32[2,2,8,16,256]{4,3,2,1,0:T(8,128)}, u32[]{:S(2)}) %copy-start.1) | copy-done | bytes 524312
  3.3 0.0 copy-start.2
  3.3 1.0 %copy-done.2 = f32[2,2,8,16,256]{4,3,2,1,0:T(8,128)S(1)} copy-done((f32[2,2,8,16,256]{4,3,2,1,0:T(8,128)S(1)}, f32[2,2,8,16,256]{4,3,2,1,0:T(8,128)}, u32[]{:S(2)}) %copy-start.2) | copy-done | bytes 524312
  4.3 0.0 copy-start.3
  4.4 0.9 %copy-done.3 = f32[15,4,2,2,16]{4,3,2,1,0:T(2,128)S(1)} copy-done((f32[15,4,2,2,16]{4,3,2,1,0:T(2,128)S(1)}, f32[15,4,2,2,16]{4,3,2,1,0:T(2,128)}, u32[]{:S(2)}) %copy-start.3) | copy-done | bytes 15384
  5.3 0.0 copy-start.4
  5.3 0.9 %copy-done.4 = f32[2,8,16,256]{3,2,1,0:T(8,128)S(1)} copy-done((f32[2,8,16,256]{3,2,1,0:T(8,128)S(1)}, f32[2,8,16,256]{3,2,1,0:T(8,128)}, u32[]{:S(2)}) %copy-start.4) | copy-done | bytes 262168
  6.2 0.0 copy-start.5
  6.2 0.9 %copy-done.5 = f32[256,128]{1,0:T(8,128)S(1)} copy-done((f32[256,128]{1,0:T(8,128)S(1)}, f32[256,128]{1,0:T(8,128)}, u32[]{:S(2)}) %copy-start.5) | copy-done | bytes 131096
  7.1 0.0 copy-start.6
  7.1 0.9 %copy-done.6 = f32[144,128]{1,0:T(8,128)S(1)} copy-done((f32[144,128]{1,0:T(8,128)S(1)}, f32[144,128]{1,0:T(8,128)}, u32[]{:S(2)}) %copy-start.6) | copy-done | bytes 73752
  8.0 0.0 copy-start.7
  8.0 0.7 %copy-done.7 = s32[2,8,16]{2,1,0:T(8,128)S(1)} copy-done((s32[2,8,16]{2,1,0:T(8,128)S(1)}, s32[2,8,16]{2,1,0:T(8,128)}, u32[]{:S(2)}) %copy-start.7) | copy-done | bytes 1048
  8.7 0.0 copy-start.8
  8.7 0.7 %copy-done.8 = f32[16,4,2,2]{0,3,2,1:T(2,128)S(1)} copy-done((f32[16,4,2,2]{0,3,2,1:T(2,128)S(1)}, f32[16,4,2,2]{0,3,2,1:T(2,128)}, u32[]{:S(2)}) %copy-start.8) | copy-done | bytes 1048
  9.4 19.4 %shard_map.129 = (f32[2,2,10,16,256]{4,3,2,1,0:T(8,128)S(1)}, f32[2,10,16,256]{3,2,1,0:T(8,128)S(1)}, f32[2,2,8,16,256]{4,3,2,1,0:T(8,128)S(1)}, f32[2,10,16,128...) custom-call(f32[2,2,8,16,256]{4,3,2,1,0:T(8,128)S(1)} %copy-done.1, ...), custom_call_target="tpu_custom_call" | custom-call | tf_op jit(solution)/shard_map/pallas_call | solution.py:421
  28.7 2.4 %shard_map.130 = (f32[2,2,8,16,256]{4,3,2,1,0:T(8,128)}, f32[2,2,8,16,256]{4,3,2,1,0:T(8,128)}, f32[2,8,16,256]{3,2,1,0:T(8,128)}, f32[15,4,2,2,16]{4,3,2,1,0:T(2,128)}) custom-call(f32[2,2,10,16,256]{4,3,2,1,0:T(8,128)S(1)} %get-tuple-element.13.u2, f32[2,10,16,256]{3,2,1,0:T(8,128)S(1)} %get-tuple-element.14.d2, ...), custom_call_target="tpu_custom_call" | custom-call | tf_op jit(solution)/shard_map/pallas_call | solution.py:459
Async XLA Ops:
  0.6 0.7 %copy-start.9 = (f32[2,4]{1,0:T(2,128)S(1)}, f32[2,4]{1,0:T(2,128)}, u32[]{:S(2)}) copy-start(f32[2,4]{1,0:T(2,128)} %table_ref.3) | copy-start | bytes 100
  1.3 0.9 %copy-start = (s32[2,8,16,256]{3,2,1,0:T(8,128)S(1)}, s32[2,8,16,256]{3,2,1,0:T(8,128)}, u32[]{:S(2)}) copy-start(s32[2,8,16,256]{3,2,1,0:T(8,128)} %mat_ref.3) | copy-start | bytes 786436
  2.3 1.0 %copy-start.1 = (f32[2,2,8,16,256]{4,3,2,1,0:T(8,128)S(1)}, f32[2,2,8,16,256]{4,3,2,1,0:T(8,128)}, u32[]{:S(2)}) copy-start(f32[2,2,8,16,256]{4,3,2,1,0:T(8,128)} %disp_hbm.1) | copy-start | bytes 1572868
  3.3 1.0 %copy-start.2 = (f32[2,2,8,16,256]{4,3,2,1,0:T(8,128)S(1)}, f32[2,2,8,16,256]{4,3,2,1,0:T(8,128)}, u32[]{:S(2)}) copy-start(f32[2,2,8,16,256]{4,3,2,1,0:T(8,128)} %vel_hbm.1) | copy-start | bytes 1572868
  4.3 0.9 %copy-start.3 = (f32[15,4,2,2,16]{4,3,2,1,0:T(2,128)S(1)}, f32[15,4,2,2,16]{4,3,2,1,0:T(2,128)}, u32[]{:S(2)}) copy-start(f32[15,4,2,2,16]{4,3,2,1,0:T(2,128)} %hist_hbm.1) | copy-start | bytes 46084
  5.3 0.9 %copy-start.4 = (f32[2,8,16,256]{3,2,1,0:T(8,128)S(1)}, f32[2,8,16,256]{3,2,1,0:T(8,128)}, u32[]{:S(2)}) copy-start(f32[2,8,16,256]{3,2,1,0:T(8,128)} %dmg_hbm.1) | copy-start | bytes 786436
  6.2 0.9 %copy-start.5 = (f32[256,128]{1,0:T(8,128)S(1)}, f32[256,128]{1,0:T(8,128)}, u32[]{:S(2)}) copy-start(f32[256,128]{1,0:T(8,128)} %constant.4.clone.forward_ref) | copy-start | bytes 393220
  7.1 0.9 %copy-start.6 = (f32[144,128]{1,0:T(8,128)S(1)}, f32[144,128]{1,0:T(8,128)}, u32[]{:S(2)}) copy-start(f32[144,128]{1,0:T(8,128)} %constant.5.clone.inverse_ref) | copy-start | bytes 221188
  8.0 0.7 %copy-start.7 = (s32[2,8,16]{2,1,0:T(8,128)S(1)}, s32[2,8,16]{2,1,0:T(8,128)}, u32[]{:S(2)}) copy-start(s32[2,8,16]{2,1,0:T(8,128)} %fault_ref.1) | copy-start | bytes 3076
  8.7 0.7 %copy-start.8 = (f32[16,4,2,2]{0,3,2,1:T(2,128)S(1)}, f32[16,4,2,2]{0,3,2,1:T(2,128)}, u32[]{:S(2)}) copy-start(f32[16,4,2,2]{0,3,2,1:T(2,128)} %param.16) | copy-start | bytes 3076

commit v3 on v2

--- a/solution.py
+++ b/solution.py
@@ -44,7 +44,7 @@
     return slice(128 * lanes, 128 * lanes + 128)
 
 
-def plane(u, d, mat_ref, table_ref, s, x, h, depth):
+def plane(u, d, rate, limit, s, x, h, depth):
     zi = lax.broadcasted_iota(jnp.int32, (depth, 128), 0)
     yi = lax.broadcasted_iota(jnp.int32, (depth, 128), 1)
 
@@ -79,18 +79,18 @@
         for k in range(3):
             slope = near[2 * k] - near[2 * k + 1]
             energy = slope * slope if energy is None else energy + slope * slope
-    material = mat_ref[s, x, :, half(h)]
-    over = 0.25 * energy - class_lookup(material, table_ref, 1)
+    over = 0.25 * energy - limit[s, x, :, half(h)]
     soft = jnp.maximum(over, 0.0) + jnp.log(1.0 + jnp.exp(-jnp.abs(over)))
-    kept = (1.0 - here) * jnp.exp(-class_lookup(material, table_ref, 0) * soft)
+    kept = (1.0 - here) * jnp.exp(-rate[s, x, :, half(h)] * soft)
     return forces, 1.0 - kept
 
 
 def exchange_body(
-    n, disp_hbm, vel_hbm, dmg_hbm, mat_ref, table_ref, fault_ref, kern_ref, hist_ref,
-    forward_ref, inverse_ref,
-    u2, d2, vel, face, push2, spec_out, disp_far, vel_far, dmg_far,
+    n, disp_hbm, vel_hbm, dmg_hbm, mat_hbm, table_hbm, fault_hbm, kern_hbm, hist_hbm,
+    forward_hbm, inverse_hbm,
+    u2, d2, vel, face, push2, spec_out, disp_far, vel_far, dmg_far, rate, limit,
     u1, d1, gather1, gather2, spectra, small,
+    mat_ref, table_ref, fault_ref, kern_ref, hist_ref, forward_ref, inverse_ref,
     load_sems, halo_send, halo_recv, all_send, all_recv,
 ):
     cells = vel.shape[2]
@@ -112,9 +112,17 @@
         pltpu.make_async_copy(disp_hbm, u1.at[:, :, pl.ds(1, cells)], load_sems.at[0]),
         pltpu.make_async_copy(dmg_hbm, d1.at[:, pl.ds(1, cells)], load_sems.at[1]),
         pltpu.make_async_copy(vel_hbm, vel, load_sems.at[2]),
+        pltpu.make_async_copy(fault_hbm, fault_ref, load_sems.at[3]),
+        pltpu.make_async_copy(kern_hbm, kern_ref, load_sems.at[4]),
+        pltpu.make_async_copy(hist_hbm, hist_ref, load_sems.at[5]),
+        pltpu.make_async_copy(table_hbm, table_ref, load_sems.at[6]),
+        pltpu.make_async_copy(mat_hbm, mat_ref, load_sems.at[7]),
+        pltpu.make_async_copy(forward_hbm, forward_ref, load_sems.at[8]),
+        pltpu.make_async_copy(inverse_hbm, inverse_ref, load_sems.at[9]),
     ]
-    for copy in loads:
-        copy.start()
+    for k in (3, 4, 5, 0, 1, 2, 6, 7, 8, 9):
+        loads[k].start()
+    loads[3].wait()
 
     diagonal = lax.broadcasted_iota(jnp.int32, (depth, depth), 0) == lax.broadcasted_iota(
         jnp.int32, (depth, depth), 1
@@ -148,6 +156,8 @@
     def exchange(block):
         return jnp.where(odd, pltpu.roll(block, 1, 0), pltpu.roll(block, cells - 1, 0))
 
+    loads[4].wait()
+    loads[5].wait()
     owned, lags = kern_ref.shape[0], kern_ref.shape[3]
     real, imag = kern_ref[:, 0], kern_ref[:, 1]
     at_lag = [
@@ -192,7 +202,6 @@
     loads[0].wait()
     gather1[own, 0:128] = quarters([slip_tile(u1), sum1, exchange(sum1), packed(5)])
     loads[1].wait()
-    loads[2].wait()
 
     pl.semaphore_wait(barrier, n - 1)
 
@@ -240,9 +249,14 @@
     spread(gather1, 0)
     for copy in far1 + faces:
         copy.start()
+    for k in (2, 6, 7, 8, 9):
+        loads[k].wait()
 
     def first_step(s, x, h):
-        forces, damaged = plane(u1, d1, mat_ref, table_ref, s, x, h, depth)
+        material = mat_ref[s, x, :, half(h)]
+        rate[s, x, :, half(h)] = class_lookup(material, table_ref, 0)
+        limit[s, x, :, half(h)] = class_lookup(material, table_ref, 1)
+        forces, damaged = plane(u1, d1, rate, limit, s, x, h, depth)
         for c in range(2):
             speed = vel[c, s, x, :, half(h)] + dt * forces[c]
             vel[c, s, x, :, half(h)] = speed
@@ -298,7 +312,7 @@
     @pl.loop(0, cells)
     def _(x):
         for s in range(2):
-            forces, damaged = plane(u2, d2, mat_ref, table_ref, s, x, 1, depth)
+            forces, damaged = plane(u2, d2, rate, limit, s, x, 1, depth)
             for c in range(2):
                 speed = vel[c, s, x, :, half(1)] + dt * forces[c]
                 vel_far[c, s, x] = speed
@@ -345,7 +359,7 @@
 
 
 def finish_body(
-    u2, d2, vel, face, push2, spec, disp_far, vel_far, dmg_far, mat_ref, table_ref, hist_hbm,
+    u2, d2, vel, face, push2, spec, disp_far, vel_far, dmg_far, rate, limit, hist_hbm,
     disp_out, vel_out, dmg_out, hist_out,
     disp_near, vel_near, dmg_near, newest, sems,
 ):
@@ -379,7 +393,7 @@
     @pl.loop(0, cells)
     def _(x):
         for s in range(2):
-            forces, damaged = plane(u2, d2, mat_ref, table_ref, s, x, 0, depth)
+            forces, damaged = plane(u2, d2, rate, limit, s, x, 0, depth)
             on = lane_f == face[s, x + 1]
             for c in range(2):
                 push = jnp.where(on, push2[c, x], 0.0)
@@ -415,13 +429,16 @@
     f32 = jnp.float32
     vmem = pl.BlockSpec(memory_space=pltpu.VMEM)
     hbm = pl.BlockSpec(memory_space=pltpu.HBM)
-    smem = pl.BlockSpec(memory_space=pltpu.SMEM)
+
+    def held(array):
+        return pltpu.with_memory_space_constraint(array, pltpu.HBM)
+
     narrow = (depth, 128)
     kern = jnp.transpose(kernel, (1, 2, 3, 0))
     middle = pl.pallas_call(
         functools.partial(exchange_body, n),
         out_shape=[
-            jax.ShapeDtypeStruct(shape, f32)
+            pltpu.VMEM(shape, f32)
             for shape in (
                 (parts, strips, cells + 2, depth, rows),
                 (strips, cells + 2, depth, rows),
@@ -432,10 +449,12 @@
                 (parts, strips, cells, *narrow),
                 (parts, strips, cells, *narrow),
                 (strips, cells, *narrow),
+                damage.shape,
+                damage.shape,
             )
         ],
-        in_specs=[hbm, hbm, hbm, vmem, smem, vmem, vmem, vmem, vmem, vmem],
-        out_specs=[vmem] * 9,
+        in_specs=[hbm] * 10,
+        out_specs=[vmem] * 11,
         scratch_shapes=[
             pltpu.VMEM((parts, strips, cells + 2, depth, rows), f32),
             pltpu.VMEM((strips, cells + 2, depth, rows), f32),
@@ -443,7 +462,14 @@
             pltpu.VMEM((length, 128), f32),
             pltpu.VMEM((2, length, 128), f32),
             pltpu.VMEM((6, 2 * cells, 128), f32),
-            pltpu.SemaphoreType.DMA((3,)),
+            pltpu.VMEM(material.shape, material.dtype),
+            pltpu.SMEM(damage_table.shape, f32),
+            pltpu.VMEM(fault_rows.shape, fault_rows.dtype),
+            pltpu.VMEM(kern.shape, f32),
+            pltpu.VMEM(history.shape, f32),
+            pltpu.VMEM(forward.shape, f32),
+            pltpu.VMEM(inverse.shape, f32),
+            pltpu.SemaphoreType.DMA((10,)),
             pltpu.SemaphoreType.DMA((18,)),
             pltpu.SemaphoreType.DMA((18,)),
             pltpu.SemaphoreType.DMA((2,)),
@@ -453,15 +479,17 @@
             collective_id=0, has_side_effects=True, vmem_limit_bytes=40 * 1024 * 1024
         ),
     )(
-        displacement, velocity, damage, material, damage_table, fault_rows, kern, history,
-        jnp.asarray(forward), jnp.asarray(inverse),
+        *map(held, (
+            displacement, velocity, damage, material, damage_table, fault_rows, kern, history,
+            jnp.asarray(forward), jnp.asarray(inverse),
+        ))
     )
     return pl.pallas_call(
         finish_body,
         out_shape=tuple(
             jax.ShapeDtypeStruct(a.shape, f32) for a in (displacement, velocity, damage, history)
         ),
-        in_specs=[vmem] * 10 + [smem, hbm],
+        in_specs=[vmem] * 11 + [hbm],
         out_specs=(hbm, hbm, hbm, hbm),
         scratch_shapes=[
             pltpu.VMEM((parts, strips, cells, *narrow), f32),
@@ -471,7 +499,7 @@
             pltpu.SemaphoreType.DMA((8,)),
         ],
         compiler_params=pltpu.CompilerParams(vmem_limit_bytes=24 * 1024 * 1024),
-    )(*middle, material, damage_table, history)
+    )(*middle, held(history))
 
 
 def solution(mesh):

time: 31.6 us -> 24.3 us (0.77)
  local copies, waits for them, and re-layouts: 8.73 us -> 0 us
  Pallas kernels: 21.8 us -> 23.4 us
    unnamed x20 -> x0, local copies, waits for them, and re-layouts: 8.73 us -> none
    pallas_call x1, Pallas kernels: 2.4 us -> 4.42 us  [per_device(): pl.pallas_call(finish_body, out_shape=tuple((jax.ShapeDtypeStruct(a.shape...]
    pallas_call x1, Pallas kernels: 19.4 us -> 19 us  [per_device(): pl.pallas_call(functools.partial(exchange_body, n), out_shape=[pltpu.VMEM...]
where the time goes in v3:
time: 24.3 us; the launch traced here: 24 us
  Pallas kernels  23.4 us (96%)
  between operations  0.64 us (3%)
    pallas_call x1, Pallas kernels, per_device(): pl.pallas_call(functools.partial(exchange_body, n), out_shape=[pltpu.VMEM...  19 us
    pallas_call x1, Pallas kernels, per_device(): pl.pallas_call(finish_body, out_shape=tuple((jax.ShapeDtypeStruct(a.shape...  4.42 us

profile of v3, /device:TPU:0, one launch (start us, length us, event | category | flops | bytes accessed | tf_op | source)
XLA Modules:
  0.0 24.0 jit_solution(11089052552136608817)
XLA Ops:
  0.6 19.0 %shard_map.129 = (f32[2,2,10,16,256]{4,3,2,1,0:T(8,128)S(1)}, f32[2,10,16,256]{3,2,1,0:T(8,128)S(1)}, f32[2,2,8,16,256]{4,3,2,1,0:T(8,128)S(1)}, f32[2,10,16,128...) custom-call(f32[2,2,8,16,256]{4,3,2,1,0:T(8,128)} %disp_hbm.1, ...), custom_call_target="tpu_custom_call" | custom-call | tf_op jit(solution)/shard_map/pallas_call | solution.py:438
  19.6 4.4 %shard_map.130 = (f32[2,2,8,16,256]{4,3,2,1,0:T(8,128)}, f32[2,2,8,16,256]{4,3,2,1,0:T(8,128)}, f32[2,8,16,256]{3,2,1,0:T(8,128)}, f32[15,4,2,2,16]{4,3,2,1,0:T(2,128)}) custom-call(f32[2,2,10,16,256]{4,3,2,1,0:T(8,128)S(1)} %get-tuple-element.15.u2, f32[2,10,16,256]{3,2,1,0:T(8,128)S(1)} %get-tuple-element.16.d2, ...), custom_call_target="tpu_custom_call" | custom-call | tf_op jit(solution)/shard_map/pallas_call | solution.py:487

commit v4 on v3

--- a/solution.py
+++ b/solution.py
@@ -88,9 +88,9 @@
 def exchange_body(
     n, disp_hbm, vel_hbm, dmg_hbm, mat_hbm, table_hbm, fault_hbm, kern_hbm, hist_hbm,
     forward_hbm, inverse_hbm,
-    u2, d2, vel, face, push2, spec_out, disp_far, vel_far, dmg_far, rate, limit,
+    u2, d2, vel, face, push2, spec_out, disp_far, vel_far, dmg_far, rate, limit, hist_ref,
     u1, d1, gather1, gather2, spectra, small,
-    mat_ref, table_ref, fault_ref, kern_ref, hist_ref, forward_ref, inverse_ref,
+    mat_ref, table_ref, fault_ref, kern_ref, forward_ref, inverse_ref,
     load_sems, halo_send, halo_recv, all_send, all_recv,
 ):
     cells = vel.shape[2]
@@ -120,8 +120,54 @@
         pltpu.make_async_copy(forward_hbm, forward_ref, load_sems.at[8]),
         pltpu.make_async_copy(inverse_hbm, inverse_ref, load_sems.at[9]),
     ]
-    for k in (3, 4, 5, 0, 1, 2, 6, 7, 8, 9):
+    for k in (3, 6, 0, 1, 2, 7, 4, 5, 8, 9):
         loads[k].start()
+    pl.semaphore_wait(barrier, n - 1)
+
+    def to(device, source, target, index):
+        return pltpu.make_async_remote_copy(
+            src_ref=source, dst_ref=target, send_sem=halo_send.at[index],
+            recv_sem=halo_recv.at[index], device_id=(group, device), device_id_type=MESH,
+        )
+
+    def halo(u_from, d_from, low, u, d, h, index):
+        lanes = pl.ds(128 * h, 128)
+        everything = slice(None)
+        high = low + cells - 1
+        return [
+            to(left, u_from.at[:, :, low, everything, lanes], u.at[:, :, cells + 1, everything, lanes], index),
+            to(right, u_from.at[:, :, high, everything, lanes], u.at[:, :, 0, everything, lanes], index + 1),
+            to(left, d_from.at[:, low, everything, lanes], d.at[:, cells + 1, everything, lanes], index + 2),
+            to(right, d_from.at[:, high, everything, lanes], d.at[:, 0, everything, lanes], index + 3),
+        ]
+
+    own = pl.ds(pl.multiple_of(me * cells, cells), cells)
+
+    def spread(buffer, index):
+        @pl.loop(1, n)
+        def _(step):
+            pltpu.make_async_remote_copy(
+                src_ref=buffer.at[own], dst_ref=buffer.at[own],
+                send_sem=all_send.at[index], recv_sem=all_recv.at[index],
+                device_id=(group, lax.rem(me + step, n)), device_id_type=MESH,
+            ).start()
+
+    def all_of(buffer, index):
+        rest = buffer.at[pl.ds(0, (n - 1) * cells)]
+        return pltpu.make_async_remote_copy(
+            src_ref=rest, dst_ref=rest,
+            send_sem=all_send.at[index], recv_sem=all_recv.at[index],
+            device_id=(group, left), device_id_type=MESH,
+        )
+
+    faces = [
+        to(left, face.at[:, 1], face.at[:, cells + 1], 16),
+        to(right, face.at[:, cells], face.at[:, 0], 17),
+    ]
+    near1 = halo(disp_hbm, dmg_hbm, 0, u1, d1, 0, 0)
+    far1 = halo(disp_hbm, dmg_hbm, 0, u1, d1, 1, 4)
+    for copy in near1 + far1:
+        copy.start()
     loads[3].wait()
 
     diagonal = lax.broadcasted_iota(jnp.int32, (depth, depth), 0) == lax.broadcasted_iota(
@@ -151,6 +197,42 @@
         parts.append(jnp.zeros((128 - 2 * depth, 128), jnp.float32))
         return jnp.concatenate(parts, 0).T[:cells, :]
 
+    for copy in faces:
+        copy.start()
+    for k in (0, 1, 2, 6, 7):
+        loads[k].wait()
+
+    def first_step(s, x, h):
+        material = mat_ref[s, x, :, half(h)]
+        rate[s, x, :, half(h)] = class_lookup(material, table_ref, 0)
+        limit[s, x, :, half(h)] = class_lookup(material, table_ref, 1)
+        forces, damaged = plane(u1, d1, rate, limit, s, x, h, depth)
+        for c in range(2):
+            speed = vel[c, s, x, :, half(h)] + dt * forces[c]
+            vel[c, s, x, :, half(h)] = speed
+            u2[c, s, x + 1, :, half(h)] = u1[c, s, x + 1, :, half(h)] + dt * speed
+        d2[s, x + 1, :, half(h)] = damaged
+
+    def step_half(h, arrivals):
+        @pl.loop(0, cells // 2 - 1)
+        def _(pair):
+            for x in (2 * pair + 1, 2 * pair + 2):
+                for s in range(2):
+                    first_step(s, x, h)
+
+        for copy in arrivals:
+            copy.wait_recv()
+
+        for x in (0, cells - 1):
+            for s in range(2):
+                first_step(s, x, h)
+
+    step_half(0, near1)
+    gather2[own, :] = slip_tile(u2)
+    spread(gather2, 1)
+    near2 = halo(u2, d2, 1, u2, d2, 0, 8)
+    for copy in near2:
+        copy.start()
     odd = lax.broadcasted_iota(jnp.int32, (cells, 128), 0) % 2 == 1
 
     def exchange(block):
@@ -196,98 +278,18 @@
             lane8 < 32, a, jnp.where(lane8 < 64, b, jnp.where(lane8 < 96, c, d))
         )
 
-    own = pl.ds(pl.multiple_of(me * cells, cells), cells)
     gather1[own, 128:256] = quarters([packed(q) for q in range(4)])
     sum1 = packed(4)
-    loads[0].wait()
     gather1[own, 0:128] = quarters([slip_tile(u1), sum1, exchange(sum1), packed(5)])
-    loads[1].wait()
-
-    pl.semaphore_wait(barrier, n - 1)
-
-    def to(device, source, target, index):
-        return pltpu.make_async_remote_copy(
-            src_ref=source, dst_ref=target, send_sem=halo_send.at[index],
-            recv_sem=halo_recv.at[index], device_id=(group, device), device_id_type=MESH,
-        )
-
-    def halo(u, d, h, index):
-        lanes = pl.ds(128 * h, 128)
-        everything = slice(None)
-        return [
-            to(left, u.at[:, :, 1, everything, lanes], u.at[:, :, cells + 1, everything, lanes], index),
-            to(right, u.at[:, :, cells, everything, lanes], u.at[:, :, 0, everything, lanes], index + 1),
-            to(left, d.at[:, 1, everything, lanes], d.at[:, cells + 1, everything, lanes], index + 2),
-            to(right, d.at[:, cells, everything, lanes], d.at[:, 0, everything, lanes], index + 3),
-        ]
-
-    def spread(buffer, index):
-        @pl.loop(1, n)
-        def _(step):
-            pltpu.make_async_remote_copy(
-                src_ref=buffer.at[own], dst_ref=buffer.at[own],
-                send_sem=all_send.at[index], recv_sem=all_recv.at[index],
-                device_id=(group, lax.rem(me + step, n)), device_id_type=MESH,
-            ).start()
-
-    def all_of(buffer, index):
-        rest = buffer.at[pl.ds(0, (n - 1) * cells)]
-        return pltpu.make_async_remote_copy(
-            src_ref=rest, dst_ref=rest,
-            send_sem=all_send.at[index], recv_sem=all_recv.at[index],
-            device_id=(group, left), device_id_type=MESH,
-        )
-
-    faces = [
-        to(left, face.at[:, 1], face.at[:, cells + 1], 16),
-        to(right, face.at[:, cells], face.at[:, 0], 17),
-    ]
-    near1 = halo(u1, d1, 0, 0)
-    far1 = halo(u1, d1, 1, 4)
-    for copy in near1:
-        copy.start()
+
     spread(gather1, 0)
-    for copy in far1 + faces:
-        copy.start()
-    for k in (2, 6, 7, 8, 9):
-        loads[k].wait()
-
-    def first_step(s, x, h):
-        material = mat_ref[s, x, :, half(h)]
-        rate[s, x, :, half(h)] = class_lookup(material, table_ref, 0)
-        limit[s, x, :, half(h)] = class_lookup(material, table_ref, 1)
-        forces, damaged = plane(u1, d1, rate, limit, s, x, h, depth)
-        for c in range(2):
-            speed = vel[c, s, x, :, half(h)] + dt * forces[c]
-            vel[c, s, x, :, half(h)] = speed
-            u2[c, s, x + 1, :, half(h)] = u1[c, s, x + 1, :, half(h)] + dt * speed
-        d2[s, x + 1, :, half(h)] = damaged
-
-    def step_half(h, arrivals):
-        @pl.loop(1, cells - 1)
-        def _(x):
-            for s in range(2):
-                first_step(s, x, h)
-
-        for copy in arrivals:
-            copy.wait_recv()
-
-        @pl.loop(0, 2)
-        def _(side):
-            for s in range(2):
-                first_step(s, side * (cells - 1), h)
-
-    step_half(0, near1)
-    gather2[own, :] = slip_tile(u2)
-    spread(gather2, 1)
-    near2 = halo(u2, d2, 0, 8)
-    for copy in near2:
-        copy.start()
     step_half(1, far1)
-    far2 = halo(u2, d2, 1, 12)
+    far2 = halo(u2, d2, 1, u2, d2, 1, 12)
     for copy in far2:
         copy.start()
 
+    loads[8].wait()
+    loads[9].wait()
     all_of(gather1, 0).wait_recv()
     waves = forward_ref.shape[0] // 2
     terms = gather1[:, 0:128]
@@ -309,15 +311,16 @@
         copy.wait_recv()
         copy.wait_send()
 
-    @pl.loop(0, cells)
-    def _(x):
-        for s in range(2):
-            forces, damaged = plane(u2, d2, rate, limit, s, x, 1, depth)
-            for c in range(2):
-                speed = vel[c, s, x, :, half(1)] + dt * forces[c]
-                vel_far[c, s, x] = speed
-                disp_far[c, s, x] = u2[c, s, x + 1, :, half(1)] + dt * speed
-            dmg_far[s, x] = damaged
+    @pl.loop(0, cells // 2)
+    def _(pair):
+        for x in (2 * pair, 2 * pair + 1):
+            for s in range(2):
+                forces, damaged = plane(u2, d2, rate, limit, s, x, 1, depth)
+                for c in range(2):
+                    speed = vel[c, s, x, :, half(1)] + dt * forces[c]
+                    vel_far[c, s, x] = speed
+                    disp_far[c, s, x] = u2[c, s, x + 1, :, half(1)] + dt * speed
+                dmg_far[s, x] = damaged
 
     all_of(gather2, 1).wait_recv()
     spec2 = jnp.dot(
@@ -359,19 +362,19 @@
 
 
 def finish_body(
-    u2, d2, vel, face, push2, spec, disp_far, vel_far, dmg_far, rate, limit, hist_hbm,
+    u2, d2, vel, face, push2, spec, disp_far, vel_far, dmg_far, rate, limit, hist_ref,
     disp_out, vel_out, dmg_out, hist_out,
     disp_near, vel_near, dmg_near, newest, sems,
 ):
     cells, depth = vel.shape[2], vel.shape[3]
     owned = newest.shape[1]
-    kept = hist_hbm.shape[0] - 2
+    kept = hist_ref.shape[0] - 2
     dt = time_step
     far = pl.ds(128, 128)
     near = pl.ds(0, 128)
     everything = slice(None)
     moves = [
-        pltpu.make_async_copy(hist_hbm.at[pl.ds(0, kept)], hist_out.at[pl.ds(2, kept)], sems.at[0]),
+        pltpu.make_async_copy(hist_ref.at[pl.ds(0, kept)], hist_out.at[pl.ds(2, kept)], sems.at[0]),
         pltpu.make_async_copy(disp_far, disp_out.at[:, :, :, everything, far], sems.at[1]),
         pltpu.make_async_copy(vel_far, vel_out.at[:, :, :, everything, far], sems.at[2]),
         pltpu.make_async_copy(dmg_far, dmg_out.at[:, :, everything, far], sems.at[3]),
@@ -390,26 +393,28 @@
     last.start()
     lane_f = lax.broadcasted_iota(jnp.int32, (depth, 128), 1).astype(jnp.float32)
 
-    @pl.loop(0, cells)
-    def _(x):
-        for s in range(2):
-            forces, damaged = plane(u2, d2, rate, limit, s, x, 0, depth)
-            on = lane_f == face[s, x + 1]
-            for c in range(2):
-                push = jnp.where(on, push2[c, x], 0.0)
-                speed = vel[c, s, x, :, half(0)] + dt * forces[c]
-                speed = speed + push if s == 0 else speed - push
-                vel_near[c, s, x] = speed
-                disp_near[c, s, x] = u2[c, s, x + 1, :, half(0)] + dt * speed
-            dmg_near[s, x] = damaged
+    @pl.loop(0, cells // 2)
+    def _(pair):
+        for x in (2 * pair, 2 * pair + 1):
+            for s in range(2):
+                forces, damaged = plane(u2, d2, rate, limit, s, x, 0, depth)
+                on = lane_f == face[s, x + 1]
+                for c in range(2):
+                    push = jnp.where(on, push2[c, x], 0.0)
+                    speed = vel[c, s, x, :, half(0)] + dt * forces[c]
+                    speed = speed + push if s == 0 else speed - push
+                    vel_near[c, s, x] = speed
+                    disp_near[c, s, x] = u2[c, s, x + 1, :, half(0)] + dt * speed
+                dmg_near[s, x] = damaged
+        both = pl.ds(2 * pair, 2)
         pltpu.make_async_copy(
-            disp_near.at[:, :, x], disp_out.at[:, :, x, everything, near], sems.at[5]
+            disp_near.at[:, :, both], disp_out.at[:, :, both, everything, near], sems.at[5]
         ).start()
         pltpu.make_async_copy(
-            vel_near.at[:, :, x], vel_out.at[:, :, x, everything, near], sems.at[6]
+            vel_near.at[:, :, both], vel_out.at[:, :, both, everything, near], sems.at[6]
         ).start()
         pltpu.make_async_copy(
-            dmg_near.at[:, x], dmg_out.at[:, x, everything, near], sems.at[7]
+            dmg_near.at[:, both], dmg_out.at[:, both, everything, near], sems.at[7]
         ).start()
 
     for copy in moves:
@@ -451,10 +456,11 @@
                 (strips, cells, *narrow),
                 damage.shape,
                 damage.shape,
+                history.shape,
             )
         ],
         in_specs=[hbm] * 10,
-        out_specs=[vmem] * 11,
+        out_specs=[vmem] * 12,
         scratch_shapes=[
             pltpu.VMEM((parts, strips, cells + 2, depth, rows), f32),
             pltpu.VMEM((strips, cells + 2, depth, rows), f32),
@@ -466,7 +472,6 @@
             pltpu.SMEM(damage_table.shape, f32),
             pltpu.VMEM(fault_rows.shape, fault_rows.dtype),
             pltpu.VMEM(kern.shape, f32),
-            pltpu.VMEM(history.shape, f32),
             pltpu.VMEM(forward.shape, f32),
             pltpu.VMEM(inverse.shape, f32),
             pltpu.SemaphoreType.DMA((10,)),
@@ -489,7 +494,7 @@
         out_shape=tuple(
             jax.ShapeDtypeStruct(a.shape, f32) for a in (displacement, velocity, damage, history)
         ),
-        in_specs=[vmem] * 11 + [hbm],
+        in_specs=[vmem] * 12,
         out_specs=(hbm, hbm, hbm, hbm),
         scratch_shapes=[
             pltpu.VMEM((parts, strips, cells, *narrow), f32),
@@ -499,7 +504,7 @@
             pltpu.SemaphoreType.DMA((8,)),
         ],
         compiler_params=pltpu.CompilerParams(vmem_limit_bytes=24 * 1024 * 1024),
-    )(*middle, held(history))
+    )(*middle)
 
 
 def solution(mesh):

time: 24.3 us -> 21.2 us (0.87)
  Pallas kernels: 23.4 us -> 20.4 us
    pallas_call x1, Pallas kernels: 4.42 us -> 1.51 us  [per_device(): pl.pallas_call(finish_body, out_shape=tuple((jax.ShapeDtypeStruct(a.shape...]
where the time goes in v4:
time: 21.2 us; the launch traced here: 21 us
  Pallas kernels  20.4 us (96%)
  between operations  0.64 us (3%)
    pallas_call x1, Pallas kernels, per_device(): pl.pallas_call(functools.partial(exchange_body, n), out_shape=[pltpu.VMEM...  18.9 us
    pallas_call x1, Pallas kernels, per_device(): pl.pallas_call(finish_body, out_shape=tuple((jax.ShapeDtypeStruct(a.shape...  1.51 us

profile of v4, /device:TPU:0, one launch (start us, length us, event | category | flops | bytes accessed | tf_op | source)
XLA Modules:
  0.0 21.0 jit_solution(6539318487201387126)
XLA Ops:
  0.6 18.9 %shard_map.129 = (f32[2,2,10,16,256]{4,3,2,1,0:T(8,128)S(1)}, f32[2,10,16,256]{3,2,1,0:T(8,128)S(1)}, f32[2,2,8,16,256]{4,3,2,1,0:T(8,128)S(1)}, f32[2,10,16,128...) custom-call(f32[2,2,8,16,256]{4,3,2,1,0:T(8,128)} %disp_hbm.1, ...), custom_call_target="tpu_custom_call" | custom-call | tf_op jit(solution)/shard_map/pallas_call | solution.py:443
  19.5 1.5 %shard_map.130 = (f32[2,2,8,16,256]{4,3,2,1,0:T(8,128)}, f32[2,2,8,16,256]{4,3,2,1,0:T(8,128)}, f32[2,8,16,256]{3,2,1,0:T(8,128)}, f32[15,4,2,2,16]{4,3,2,1,0:T(2,128)}) custom-call(f32[2,2,10,16,256]{4,3,2,1,0:T(8,128)S(1)} %get-tuple-element.16.u2, f32[2,10,16,256]{3,2,1,0:T(8,128)S(1)} %get-tuple-element.17.d2, ...), custom_call_target="tpu_custom_call" | custom-call | tf_op jit(solution)/shard_map/pallas_call | solution.py:492

commit v5 on v4

--- a/solution.py
+++ b/solution.py
@@ -199,45 +199,7 @@
 
     for copy in faces:
         copy.start()
-    for k in (0, 1, 2, 6, 7):
-        loads[k].wait()
-
-    def first_step(s, x, h):
-        material = mat_ref[s, x, :, half(h)]
-        rate[s, x, :, half(h)] = class_lookup(material, table_ref, 0)
-        limit[s, x, :, half(h)] = class_lookup(material, table_ref, 1)
-        forces, damaged = plane(u1, d1, rate, limit, s, x, h, depth)
-        for c in range(2):
-            speed = vel[c, s, x, :, half(h)] + dt * forces[c]
-            vel[c, s, x, :, half(h)] = speed
-            u2[c, s, x + 1, :, half(h)] = u1[c, s, x + 1, :, half(h)] + dt * speed
-        d2[s, x + 1, :, half(h)] = damaged
-
-    def step_half(h, arrivals):
-        @pl.loop(0, cells // 2 - 1)
-        def _(pair):
-            for x in (2 * pair + 1, 2 * pair + 2):
-                for s in range(2):
-                    first_step(s, x, h)
-
-        for copy in arrivals:
-            copy.wait_recv()
-
-        for x in (0, cells - 1):
-            for s in range(2):
-                first_step(s, x, h)
-
-    step_half(0, near1)
-    gather2[own, :] = slip_tile(u2)
-    spread(gather2, 1)
-    near2 = halo(u2, d2, 1, u2, d2, 0, 8)
-    for copy in near2:
-        copy.start()
-    odd = lax.broadcasted_iota(jnp.int32, (cells, 128), 0) % 2 == 1
-
-    def exchange(block):
-        return jnp.where(odd, pltpu.roll(block, 1, 0), pltpu.roll(block, cells - 1, 0))
-
+    loads[0].wait()
     loads[4].wait()
     loads[5].wait()
     owned, lags = kern_ref.shape[0], kern_ref.shape[3]
@@ -272,39 +234,79 @@
         second = pltpu.roll(small[q, cells : 2 * cells], depth, 1)
         return jnp.where(lane8 < depth, small[q, 0:cells], second)
 
-    def quarters(parts):
-        a, b, c, d = [p if i == 0 else pltpu.roll(p, 32 * i, 1) for i, p in enumerate(parts)]
-        return jnp.where(
-            lane8 < 32, a, jnp.where(lane8 < 64, b, jnp.where(lane8 < 96, c, d))
-        )
-
-    gather1[own, 128:256] = quarters([packed(q) for q in range(4)])
-    sum1 = packed(4)
-    gather1[own, 0:128] = quarters([slip_tile(u1), sum1, exchange(sum1), packed(5)])
-
+    sum1, sum2 = packed(4), packed(5)
+    tile = jnp.where(lane8 < 32, slip_tile(u1), pltpu.roll(sum1, 32, 1))
+    tile = jnp.where(lane8 < 64, tile, pltpu.roll(sum2, 64, 1))
+    for q in range(4):
+        spreadable = packed(q)
+        for c in range(2):
+            column = spreadable[:, c * depth : c * depth + 1]
+            tile = jnp.where(lane8 == 96 + 2 * q + c, column, tile)
+    gather1[own, :] = jnp.where(lane8 < 104, tile, 0.0)
     spread(gather1, 0)
-    step_half(1, far1)
+    for k in (1, 2, 6, 7):
+        loads[k].wait()
+
+    def first_step(s, x, h):
+        material = mat_ref[s, x, :, half(h)]
+        rate[s, x, :, half(h)] = class_lookup(material, table_ref, 0)
+        limit[s, x, :, half(h)] = class_lookup(material, table_ref, 1)
+        forces, damaged = plane(u1, d1, rate, limit, s, x, h, depth)
+        for c in range(2):
+            speed = vel[c, s, x, :, half(h)] + dt * forces[c]
+            vel[c, s, x, :, half(h)] = speed
+            u2[c, s, x + 1, :, half(h)] = u1[c, s, x + 1, :, half(h)] + dt * speed
+        d2[s, x + 1, :, half(h)] = damaged
+
+    def inner(h):
+        @pl.loop(0, cells // 2 - 1)
+        def _(pair):
+            for x in (2 * pair + 1, 2 * pair + 2):
+                for s in range(2):
+                    first_step(s, x, h)
+
+    def outer(h, arrivals):
+        for copy in arrivals:
+            copy.wait_recv()
+        for x in (0, cells - 1):
+            for s in range(2):
+                first_step(s, x, h)
+
+    inner(0)
+    outer(0, near1)
+    gather2[own, :] = slip_tile(u2)
+    spread(gather2, 1)
+    near2 = halo(u2, d2, 1, u2, d2, 0, 8)
+    for copy in near2:
+        copy.start()
+    outer(1, far1)
     far2 = halo(u2, d2, 1, u2, d2, 1, 12)
     for copy in far2:
         copy.start()
+    inner(1)
 
     loads[8].wait()
     loads[9].wait()
     all_of(gather1, 0).wait_recv()
     waves = forward_ref.shape[0] // 2
-    terms = gather1[:, 0:128]
-    kernels = gather1[:, 128:256]
+    terms = gather1[...]
     spec1 = jnp.dot(forward_ref[...], terms, precision=HIGHEST, preferred_element_type=jnp.float32)
     cur, cur_s = spec1[:waves], spec1[waves:]
-    kr0, ki0 = kernels, pltpu.roll(kernels, 96, 1)
-    kr1, ki1 = pltpu.roll(kernels, 64, 1), pltpu.roll(kernels, 32, 1)
-    tract1 = kr0 * cur + ki0 * cur_s + pltpu.roll(terms, 96, 1)
-    tract1_s = kr0 * cur_s - ki0 * cur + pltpu.roll(terms, 64, 1)
+    first_part = lax.broadcasted_iota(jnp.int32, (waves, 128), 1) < depth
+    kr0, ki0, kr1, ki1 = [
+        jnp.where(first_part, terms[:, at : at + 1], terms[:, at + 1 : at + 2])
+        for at in (96, 98, 100, 102)
+    ]
+    odd = lax.broadcasted_iota(jnp.int32, (waves, 128), 0) % 2 == 1
+    sums1, sums2 = pltpu.roll(terms, 96, 1), pltpu.roll(terms, 64, 1)
+    sums1_s = jnp.where(odd, pltpu.roll(sums1, 1, 0), pltpu.roll(sums1, waves - 1, 0))
+    tract1 = kr0 * cur + ki0 * cur_s + sums1
+    tract1_s = kr0 * cur_s - ki0 * cur + sums1_s
     row = lax.broadcasted_iota(jnp.int32, (waves, 128), 0)
     wide = lax.broadcasted_iota(jnp.int32, (waves, 128), 1)
     back1 = 2.0 * dt * dt * jnp.where(row == 1, 0.0, tract1)
     back1_s = 2.0 * dt * dt * jnp.where(row == 0, 0.0, tract1_s)
-    partial2 = kr1 * cur + ki1 * cur_s + pltpu.roll(terms, 32, 1)
+    partial2 = kr1 * cur + ki1 * cur_s + sums2
     spectra[0] = cur
 
     for copy in near2 + far2:
@@ -464,7 +466,7 @@
         scratch_shapes=[
             pltpu.VMEM((parts, strips, cells + 2, depth, rows), f32),
             pltpu.VMEM((strips, cells + 2, depth, rows), f32),
-            pltpu.VMEM((length, 256), f32),
+            pltpu.VMEM((length, 128), f32),
             pltpu.VMEM((length, 128), f32),
             pltpu.VMEM((2, length, 128), f32),
             pltpu.VMEM((6, 2 * cells, 128), f32),

time: 21.2 us -> 20.4 us (0.962)
  Pallas kernels: 20.4 us -> 19.6 us
    pallas_call x1, Pallas kernels: 18.9 us -> 18 us  [per_device(): pl.pallas_call(functools.partial(exchange_body, n), out_shape=[pltpu.VMEM...]
where the time goes in v5:
time: 20.4 us; the launch traced here: 20.2 us
  Pallas kernels  19.6 us (96%)
  between operations  0.64 us (3%)
    pallas_call x1, Pallas kernels, per_device(): pl.pallas_call(functools.partial(exchange_body, n), out_shape=[pltpu.VMEM...  18 us
    pallas_call x1, Pallas kernels, per_device(): pl.pallas_call(finish_body, out_shape=tuple((jax.ShapeDtypeStruct(a.shape...  1.51 us

profile of v5, /device:TPU:0, one launch (start us, length us, event | category | flops | bytes accessed | tf_op | source)
XLA Modules:
  0.0 20.2 jit_solution(4551350892209145180)
XLA Ops:
  0.6 18.0 %shard_map.129 = (f32[2,2,10,16,256]{4,3,2,1,0:T(8,128)S(1)}, f32[2,10,16,256]{3,2,1,0:T(8,128)S(1)}, f32[2,2,8,16,256]{4,3,2,1,0:T(8,128)S(1)}, f32[2,10,16,128...) custom-call(f32[2,2,8,16,256]{4,3,2,1,0:T(8,128)} %disp_hbm.1, ...), custom_call_target="tpu_custom_call" | custom-call | tf_op jit(solution)/shard_map/pallas_call | solution.py:445
  18.7 1.5 %shard_map.130 = (f32[2,2,8,16,256]{4,3,2,1,0:T(8,128)}, f32[2,2,8,16,256]{4,3,2,1,0:T(8,128)}, f32[2,8,16,256]{3,2,1,0:T(8,128)}, f32[15,4,2,2,16]{4,3,2,1,0:T(2,128)}) custom-call(f32[2,2,10,16,256]{4,3,2,1,0:T(8,128)S(1)} %get-tuple-element.16.u2, f32[2,10,16,256]{3,2,1,0:T(8,128)S(1)} %get-tuple-element.17.d2, ...), custom_call_target="tpu_custom_call" | custom-call | tf_op jit(solution)/shard_map/pallas_call | solution.py:494
